TPU v7x, 128 devices: a whole 4x4x4 slice. The times are simulated.
128 devices in a mesh: gx: 16 (over z, y), gy: 8 (over x, core).
Axes of the slice: x: 4, y: 4, z: 4, core: 2. Of those that a mesh axis runs over, the one named last changes fastest.
Arguments:
- ocean_temp: float32 [64, 64, 2048], P(None, 'gy', 'gx'), may hold values from -2 to 1.5
- ocean_salt: float32 [64, 64, 2048], P(None, 'gy', 'gx'), may hold values from 33.8 to 34.8
- wet_mask: int32 [64, 64, 2048], P(None, 'gy', 'gx'), may hold values 0 or 1
- vertical_mix: float32 [64, 2048], P('gy', 'gx'), may hold values from 0.05 to 0.3
- friction: float32 [64, 2048], P('gy', 'gx'), may hold values from 0.5 to 5
- pressure: float32 [64, 2048], P('gy', 'gx'), may hold values from 200 to 1500
- pair_column: int32 [65536, 128], P(('gx', 'gy')), may hold values from 0 to 1023
- pair_weight: float32 [65536, 128], P(('gx', 'gy')), may hold values from 0.05 to 1
- block_owner: int32 [65536, 1], P(('gx', 'gy')), may hold values from 0 to 127; in each aligned block of 512 rows (0 to 511, 512 to 1023, ...) at most 8 rows name the same one
- block_target: int32 [65536], P(('gx', 'gy')), may hold values from 0 to 31
- enthalpy: float32 [40, 524288], P(None, ('gx', 'gy')), may hold values from -1 to 0.2
- surface_enthalpy: float32 [524288], P(('gx', 'gy')), may hold values from -1.5 to -0.5
- transition_layer: int32 [524288], P(('gx', 'gy')), may hold values from 0 to 40
- column_area: float32 [524288], P(('gx', 'gy')), may hold values from 0.5 to 2
Outputs:
- new_temp: float32 [64, 64, 2048], P(None, 'gy', 'gx')
- new_salt: float32 [64, 64, 2048], P(None, 'gy', 'gx')
- new_enthalpy: float32 [40, 524288], P(None, ('gx', 'gy'))
- ice_melt: float32 [524288], P(('gx', 'gy'))
Inputs may be any that keep to these rules, and one draw needn't show every extreme that they name: `block_owner`: of the 512 blocks of one device at most 8 name the same owner, and some owner gets exactly 8 of them.
All inputs are finite; a program needn't handle non-finite values. No bound on the sum of `wet_mask` on one device may be relied on, other than what follows from the above.
Results may differ from a plain program's by a relative error of at most 0.000059.
Values sent between devices are 32-bit elements; how exact they have to be, the bound alone decides.
No kernel may reach another device: no remote copies, remote signals or barrier semaphores. Data moves between devices by JAX's collectives and lax.ppermute only.
A program may use at most 64 MiB of HBM per device.

v0:
```python
import jax
import jax.numpy as jnp
from jax import lax
from jax.sharding import PartitionSpec as P

mixing_rate = 0.2
liquidus_slope = -0.0573
liquidus_base = 0.0832
liquidus_depth = -0.000753
latent_ratio = 4.0
salt_ratio = 35.0
relax_rate = 0.1
cold_rate = 2.0
temperate_rate = 0.2


def padded(block, sides, width):
    for axis, dim in sides:
        count = lax.axis_size(axis)
        forward = [(i, i + 1) for i in range(count - 1)]
        backward = [(target, source) for source, target in forward]
        low = lax.ppermute(
            lax.slice_in_dim(block, block.shape[dim] - width, None, axis=dim), axis, forward
        )
        high = lax.ppermute(lax.slice_in_dim(block, 0, width, axis=dim), axis, backward)
        block = jnp.concatenate([low, block, high], axis=dim)
    return block


def spread_sideways(extended, wet_ext):
    middle = extended[:, :, 1:-1, 1:-1]
    wet_mid = wet_ext[:, 1:-1, 1:-1]
    height = middle.shape[2]
    breadth = middle.shape[3]
    change = jnp.zeros_like(middle)
    for row_off, col_off in ((0, 1), (2, 1), (1, 0), (1, 2)):
        beside = extended[:, :, row_off : row_off + height, col_off : col_off + breadth]
        wet_beside = wet_ext[:, row_off : row_off + height, col_off : col_off + breadth]
        change = change + (wet_mid * wet_beside)[None] * (beside - middle)
    return middle + mixing_rate * change


def mix_vertical(fields, wetness, vertical_mix):
    link = wetness[:-1] * wetness[1:]
    level_flux = vertical_mix[None, None] * link[None] * (fields[:, 1:] - fields[:, :-1])
    return (
        fields
        + jnp.pad(level_flux, ((0, 0), (0, 1), (0, 0), (0, 0)))
        - jnp.pad(level_flux, ((0, 0), (1, 0), (0, 0), (0, 0)))
    )


def shelf_melt(surface_temp, surface_salt, friction, pressure, wet_top):
    heat_gain = jnp.where(wet_top > 0, friction, 1.0)
    salt_safe = jnp.where(wet_top > 0, surface_salt, 34.0)
    salt_gain = heat_gain / salt_ratio
    curvature = heat_gain * liquidus_slope
    linear = (
        heat_gain * (surface_temp - liquidus_base - liquidus_depth * pressure)
        + latent_ratio * salt_gain
    )
    constant = latent_ratio * salt_gain * salt_safe
    boundary_salt = (
        2.0 * constant / (linear + jnp.sqrt(linear * linear - 4.0 * curvature * constant))
    )
    boundary_temp = liquidus_slope * boundary_salt + liquidus_base + liquidus_depth * pressure
    heat_flux = heat_gain * (surface_temp - boundary_temp) * wet_top
    salt_flux = salt_gain * (salt_safe - boundary_salt) * wet_top
    return (heat_flux, salt_flux, boundary_temp * wet_top)


def ocean_update(extended, wet_ext, vertical_mix, friction, pressure):
    fields = spread_sideways(extended, wet_ext)
    wetness = wet_ext[:, 1:-1, 1:-1]
    fields = mix_vertical(fields, wetness, vertical_mix)
    heat_flux, salt_flux, base_temp = shelf_melt(
        fields[0, 0], fields[1, 0], friction, pressure, wetness[0]
    )
    top_level = jnp.stack(
        [fields[0, 0] - relax_rate * heat_flux, fields[1, 0] - relax_rate * salt_flux]
    )
    fields = fields.at[:, 0].set(top_level)
    return (fields, heat_flux / latent_ratio, base_temp)


def solve_columns(enthalpy, transition_layer, surface_enthalpy, cover_sum, base_sum):
    layers = enthalpy.shape[0]
    level = jnp.arange(layers, dtype=jnp.int32)[:, None]
    rate = jnp.where(level < transition_layer[None, :], cold_rate, temperate_rate).astype(
        jnp.float32
    )
    inner = 0.5 * (rate[:-1] + rate[1:])
    zero_row = jnp.zeros_like(rate[:1])
    lower = jnp.concatenate([rate[:1], inner], axis=0)
    upper = jnp.concatenate([inner, cover_sum[None, :]], axis=0)
    diagonal = 1.0 + lower + upper
    below = -jnp.concatenate([zero_row, inner], axis=0)
    above = -jnp.concatenate([inner, zero_row], axis=0)
    right_side = enthalpy.at[0].add(rate[0] * surface_enthalpy).at[layers - 1].add(base_sum)

    def forward(carry, items):
        ratio_prev, value_prev = carry
        diag_now, below_now, above_now, side_now = items
        pivot = diag_now - below_now * ratio_prev
        ratio_now = above_now / pivot
        value_now = (side_now - below_now * value_prev) / pivot
        return ((ratio_now, value_now), (ratio_now, value_now))

    start = (jnp.zeros_like(rate[0]), jnp.zeros_like(rate[0]))
    unused, (ratios, values) = lax.scan(forward, start, (diagonal, below, above, right_side))

    def backward(next_value, items):
        ratio_now, value_now = items
        result = value_now - ratio_now * next_value
        return (result, result)

    unused_last, solved = lax.scan(
        backward, jnp.zeros_like(rate[0]), (ratios, values), reverse=True
    )
    return solved


def local(
    ocean_temp,
    ocean_salt,
    wet_mask,
    vertical_mix,
    friction,
    pressure,
    pair_column,
    pair_weight,
    block_owner,
    block_target,
    enthalpy,
    surface_enthalpy,
    transition_layer,
    column_area,
):
    wetness = wet_mask.astype(jnp.float32)
    fields = jnp.stack([ocean_temp, ocean_salt])
    melt_total = jnp.zeros_like(friction)
    base_total = jnp.zeros_like(friction)
    wet_ext = padded(wetness, (("gx", 2), ("gy", 1)), 1)
    for step in range(2):
        extended = padded(fields, (("gx", 3), ("gy", 2)), 1)
        fields, melt_rate, base_temp = ocean_update(
            extended, wet_ext, vertical_mix, friction, pressure
        )
        melt_total = melt_total + melt_rate
        base_total = base_total + base_temp
    mean_melt = (0.5 * melt_total).reshape(-1)
    mean_base = (0.5 * base_total).reshape(-1)
    count_x = lax.axis_size("gx")
    count_y = lax.axis_size("gy")
    devices = count_x * count_y
    blocks_here = pair_column.shape[0]
    block_width = pair_column.shape[1]
    capacity = max(2, (2 * blocks_here + devices - 1) // devices)
    owner = block_owner[:, 0]
    owner_hot = (owner[:, None] == jnp.arange(devices, dtype=jnp.int32)[None, :]).astype(jnp.int32)
    rank = jnp.sum(jnp.cumsum(owner_hot, axis=0) * owner_hot, axis=1) - 1
    slot = owner * capacity + rank
    payload = jnp.stack(
        [pair_weight * mean_melt[pair_column], pair_weight * mean_base[pair_column], pair_weight],
        axis=1,
    )
    send_values = jnp.zeros((devices * capacity, 3, block_width), jnp.float32).at[slot].set(payload)
    send_target = (
        jnp.full((devices * capacity,), -1.0, jnp.float32)
        .at[slot]
        .set(block_target.astype(jnp.float32))
    )
    got_values, got_target = (
        lax.all_to_all(
            send_values.reshape(devices, capacity, 3, block_width),
            ("gx", "gy"),
            split_axis=0,
            concat_axis=0,
            tiled=True,
        ),
        lax.all_to_all(
            send_target.reshape(devices, capacity),
            ("gx", "gy"),
            split_axis=0,
            concat_axis=0,
            tiled=True,
        ),
    )
    flat_values = got_values.reshape(devices * capacity, 3 * block_width)
    flat_target = got_target.reshape(devices * capacity)
    ice_cols = enthalpy.shape[1]
    ice_blocks = ice_cols // block_width
    target_hot = (
        flat_target[None, :] == jnp.arange(ice_blocks, dtype=jnp.int32).astype(jnp.float32)[:, None]
    ).astype(jnp.float32)
    gathered = jnp.dot(
        target_hot, flat_values, precision=lax.Precision.HIGHEST, preferred_element_type=jnp.float32
    )
    gathered = gathered.reshape(ice_blocks, 3, block_width)
    melt_sum = gathered[:, 0, :].reshape(ice_cols) / column_area
    base_sum = gathered[:, 1, :].reshape(ice_cols) / column_area
    cover_sum = gathered[:, 2, :].reshape(ice_cols) / column_area
    new_enthalpy = solve_columns(enthalpy, transition_layer, surface_enthalpy, cover_sum, base_sum)
    return (fields[0], fields[1], new_enthalpy, melt_sum)


def solution(mesh):
    return jax.shard_map(
        local,
        mesh=mesh,
        in_specs=(
            P(None, "gy", "gx"),
            P(None, "gy", "gx"),
            P(None, "gy", "gx"),
            P("gy", "gx"),
            P("gy", "gx"),
            P("gy", "gx"),
            P(("gx", "gy"), None),
            P(("gx", "gy"), None),
            P(("gx", "gy"), None),
            P(("gx", "gy")),
            P(None, ("gx", "gy")),
            P(("gx", "gy")),
            P(("gx", "gy")),
            P(("gx", "gy")),
        ),
        out_specs=(
            P(None, "gy", "gx"),
            P(None, "gy", "gx"),
            P(None, ("gx", "gy")),
            P(("gx", "gy")),
        ),
        check_vma=False,
    )
```

profile of v0, /device:TPU:1, one launch (start us, length us, event | category | flops | bytes accessed | tf_op | source)
XLA Modules:
  0.0 755.9 jit_solution(10046899376783281334)
XLA Ops:
  0.7 1.1 copy.70
  1.8 1.2 convert_element_type.25
  3.8 4.0 collective-permute-start
  7.9 1.3 collective-permute-start.1
  9.2 1.1 fusion.8
  10.3 4.1 collective-permute-start.3
  14.5 1.3 collective-permute-start.4
  16.5 2.4 scatter_custom_fusion
  19.7 14.6 %all-to-all-start = ((f32[128,1,8]{2,1,0:T(1,128)}), f32[128,1,8]{2,1,0:T(1,128)}, u32[]{:S(2)}, u32[]{:S(2)}) async-start(f32[128,1,8]{2,1,0:T(1,128)} %bitcast.23), calls=%async_computation | async-start | bytes 131072 | tf_op jit(solution)/shard_map/all_to_all | solution.py:181
  34.2 1.0 fusion.39
  35.8 3.5 collective-permute-start.2
  39.4 1.9 collective-permute-start.6
  42.2 3.6 collective-permute-start.5
  45.8 1.9 collective-permute-start.7
  48.4 3.8 collective-permute-done.7
  52.1 1.1 fusion.27
  53.3 1.1 pad_subtract_fusion.1
  54.7 3.1 collective-permute-start.8
  57.8 1.3 collective-permute-start.9
  60.1 6.9 collective-permute-done.8
  66.9 4.1 collective-permute-done.9
  71.9 5.0 collective-permute-start.10
  77.0 2.1 collective-permute-start.11
  79.8 3.5 collective-permute-done.11
  83.3 1.0 fusion.14
  84.4 1.0 pad_subtract_fusion
  86.2 260.7 %gather_fusion = f32[65536]{0:T(1024)S(1)} fusion(f32[1024]{0:T(1024)S(1)} %get-tuple-element.282, s32[65536]{0:T(1024)S(1)} %fusion.39), kind=kCustom, calls=%fused_computation | custom fusion | bytes 786432 | tf_op jit(solution)/shard_map/gather | solution.py:164
  346.9 260.7 %gather_fusion.1 = f32[65536]{0:T(1024)S(1)} fusion(f32[1024]{0:T(1024)S(1)} %get-tuple-element.299, s32[65536]{0:T(1024)S(1)} %fusion.39), kind=kCustom, calls=%fused_computation.1 | custom fusion | bytes 786432 | tf_op jit(solution)/shard_map/gather | solution.py:164
  608.5 13.6 %scatter_fusion = f32[1024,3,128]{2,1,0:T(4,128)S(1)} fusion(f32[1024,3,128]{2,1,0:T(4,128)S(1)} %broadcast_in_dim.70, s32[512]{0:T(512)S(1)} %bitcast.226, f32[512,3,128]{2,1,0:T(4,128)S(1)} %copy.31), kind=kCustom, calls=%fused_computation.3 | custom fusion | bytes 2361344 | tf_op jit(solution)/shard_map/scatter | solution.py:167
  622.1 1.3 copy.33
  623.4 9.9 %all-to-all-start.1 = ((f32[128,8,3,128]{3,1,2,0:T(8,128)}), f32[128,8,3,128]{3,1,2,0:T(8,128)S(1)}, u32[]{:S(2)}, u32[]{:S(2)}) async-start(f32[128,8,3,128]{3,1,2,0:T(8,128)} %copy.33), calls=%async_computation.1 | async-start | bytes 3145728 | tf_op jit(solution)/shard_map/all_to_all | solution.py:174
  633.4 1.6 scatter-add.6
  636.5 1.6 reduce.11
  639.1 19.1 %all-to-all-done.1 = f32[128,8,3,128]{3,1,2,0:T(8,128)S(1)} async-done(((f32[128,8,3,128]{3,1,2,0:T(8,128)}), f32[128,8,3,128]{3,1,2,0:T(8,128)S(1)}, u32[]{:S(2)}, u32[]{:S(2)}) %all-to-all-start.1) | async-done | bytes 1572896 | tf_op jit(solution)/shard_map/all_to_all | solution.py:174
  661.1 1.6 scatter-add.9
  663.1 72.8 %while.38 = (s32[]{:T(128)}, f32[4096]{0:T(1024)S(1)}, f32[4096]{0:T(1024)S(1)}, f32[40,4096]{1,0:T(8,128)S(1)}, f32[40,4096]{1,0:T(8,128)S(1)}, /*index=5*/f32[...) while((s32[]{:T(128)}, f32[4096]{0:T(1024)S(1)}, ...), condition=%wide.region_6.7_spmd.clone, body=%wide.region_5.6_spmd.clone.sunk | while | flops 32771 | bytes 327815 | solution.py:110
  663.1 0.9 constant_dynamic-slice_fusion.9
  664.9 0.9 constant_dynamic-slice_fusion.9
  666.8 0.9 constant_dynamic-slice_fusion.9
  668.6 0.9 constant_dynamic-slice_fusion.9
  670.4 0.9 constant_dynamic-slice_fusion.9
  672.2 0.9 constant_dynamic-slice_fusion.9
  674.0 0.9 constant_dynamic-slice_fusion.9
  675.9 0.9 constant_dynamic-slice_fusion.9
  677.7 0.9 constant_dynamic-slice_fusion.9
  679.5 0.9 constant_dynamic-slice_fusion.9
  681.3 0.9 constant_dynamic-slice_fusion.9
  683.1 0.9 constant_dynamic-slice_fusion.9
  685.0 0.9 constant_dynamic-slice_fusion.9
  686.8 0.9 constant_dynamic-slice_fusion.9
  688.6 0.9 constant_dynamic-slice_fusion.9
  690.4 0.9 constant_dynamic-slice_fusion.9
  692.2 0.9 constant_dynamic-slice_fusion.9
  694.1 0.9 constant_dynamic-slice_fusion.9
  695.9 0.9 constant_dynamic-slice_fusion.9
  697.7 0.9 constant_dynamic-slice_fusion.9
  699.5 0.9 constant_dynamic-slice_fusion.9
  701.3 0.9 constant_dynamic-slice_fusion.9
  703.2 0.9 constant_dynamic-slice_fusion.9
  705.0 0.9 constant_dynamic-slice_fusion.9
  708.6 0.9 constant_dynamic-slice_fusion.9
  714.1 0.9 constant_dynamic-slice_fusion.9
  719.5 0.9 constant_dynamic-slice_fusion.9
  736.0 19.0 %while.39 = (s32[]{:T(128)}, f32[4096]{0:T(1024)S(1)}, f32[40,4096]{1,0:T(8,128)S(1)}, f32[40,4096]{1,0:T(8,128)S(1)}, f32[40,4096]{1,0:T(8,128)S(1)}, /*index=5*/s32[]{:T(128)}, s32[]{:T(128)}, s32[]{:T(128)}) while((s32[]{:T(128)}, f32[4096]{0:T(1024)S(1)}, f32[40,4096]{1,0:T(8,128)S(1)}, f32[40,4096]{1,0:T(8,128)S(1)}, ...), condition=%wide.region_8.9_spmd.clone, body=%wide.region_7.8_spmd.clone.sunk | while | flops 12292 | bytes 163955 | solution.py:117
  (405 shorter events, 78.0 us)
Async XLA Ops:
  0.6 8.5 %copy-start.2 = (f32[64,8,128]{2,1,0:T(8,128)S(1)}, f32[64,8,128]{2,1,0:T(8,128)}, u32[]{:S(2)}) copy-start(f32[64,8,128]{2,1,0:T(8,128)} %param.26) | copy-start | bytes 786436
  0.6 8.5 %copy-start.3 = (f32[64,8,128]{2,1,0:T(8,128)S(1)}, f32[64,8,128]{2,1,0:T(8,128)}, u32[]{:S(2)}) copy-start(f32[64,8,128]{2,1,0:T(8,128)} %param.27) | copy-start | bytes 786436
  1.8 77.3 %copy-start.8 = (f32[40,4096]{1,0:T(8,128)}, f32[40,4096]{1,0:T(8,128)S(1)}, u32[]{:S(2)}) copy-start(f32[40,4096]{1,0:T(8,128)S(1)} %copy.70) | copy-start | bytes 1966084
  1.8 14.0 %copy-start.15 = (s32[512,1]{0,1:T(1,128)S(1)}, s32[512,1]{0,1:T(1,128)}, u32[]{:S(2)}) copy-start(s32[512,1]{0,1:T(1,128)} %param.34) | copy-start | bytes 6148
  3.8 31.5 %collective-permute-start = (f32[64,8,1]{2,1,0:T(8,128)}, f32[64,8,1]{2,1,0:T(8,128)S(1)}, u32[]{:S(2)}, u32[]{:S(2)}) collective-permute-start(f32[64,8,1]{2,1,0:T(8,128)} %get-tuple-element.318), channel_id=1, source_target_pairs={{0,8},{8,16},{16,24},{24,32},{32,40},{40,48},{48,56},{56,64},{64,7... | collective-permute-start | bytes 6152 | tf_op jit(solution)/shard_map/ppermute | solution.py:22
  7.9 27.5 %collective-permute-start.1 = (f32[64,8,1]{2,1,0:T(8,128)}, f32[64,8,1]{2,1,0:T(8,128)S(1)}, u32[]{:S(2)}, u32[]{:S(2)}) collective-permute-start(f32[64,8,1]{2,1,0:T(8,128)} %get-tuple-element.319), channel_id=1, source_target_pairs={{8,0},{16,8},{24,16},{32,24},{40,32},{48,40},{56,48},{64,56},{72,6... | collective-permute-start | bytes 6152 | tf_op jit(solution)/shard_map/ppermute | solution.py:25
  9.2 7.3 copy-start.24
  10.3 25.0 %copy-start.23 = (f32[8,128]{1,0:T(8,128)S(1)}, f32[8,128]{1,0:T(8,128)}, u32[]{:S(2)}) copy-start(f32[8,128]{1,0:T(8,128)} %param.29) | copy-start | bytes 12292
  10.3 31.0 %collective-permute-start.3 = (f32[2,64,8,1]{3,2,1,0:T(8,128)}, f32[2,64,8,1]{3,2,1,0:T(8,128)S(1)}, u32[]{:S(2)}, u32[]{:S(2)}) collective-permute-start(f32[2,64,8,1]{3,2,1,0:T(8,128)} %get-tuple-element.314), channel_id=1, source_target_pairs={{0,8},{8,16},{16,24},{24,32},{32,40},{40,48},{48,56},{56,64},{64,7... | collective-permute-start | bytes 12296 | tf_op jit(solution)/shard_map/ppermute | solution.py:22
  14.5 26.8 %collective-permute-start.4 = (f32[2,64,8,1]{3,2,1,0:T(8,128)}, f32[2,64,8,1]{3,2,1,0:T(8,128)S(1)}, u32[]{:S(2)}, u32[]{:S(2)}) collective-permute-start(f32[2,64,8,1]{3,2,1,0:T(8,128)} %get-tuple-element.315), channel_id=1, source_target_pairs={{8,0},{16,8},{24,16},{32,24},{40,32},{48,40},{56,48},{64,56},{72,6... | collective-permute-start | bytes 12296 | tf_op jit(solution)/shard_map/ppermute | solution.py:25
  16.5 25.7 %copy-start.21 = (s32[512,1]{0,1:T(1,128)}, s32[512,1]{0,1:T(1,128)S(1)}, u32[]{:S(2)}) copy-start(s32[512,1]{0,1:T(1,128)S(1)} %compare_select_fusion.1) | copy-start | bytes 6148
  19.7 603.7 %all-to-all-start = ((f32[128,1,8]{2,1,0:T(1,128)}), f32[128,1,8]{2,1,0:T(1,128)}, u32[]{:S(2)}, u32[]{:S(2)}) async-start(f32[128,1,8]{2,1,0:T(1,128)} %bitcast.23), calls=%async_computation | async-start | bytes 131072 | tf_op jit(solution)/shard_map/all_to_all | solution.py:181
  35.8 12.0 %collective-permute-start.2 = (f32[64,1,130]{2,1,0:T(1,128)S(1)}, f32[64,1,130]{2,1,0:T(1,128)S(1)}, u32[]{:S(2)}, u32[]{:S(2)}) collective-permute-start(f32[64,1,130]{2,1,0:T(1,128)S(1)} %get-tuple-element.303), channel_id=1, source_target_pairs={{0,1},{1,2},{2,3},{3,4},{4,5},{5,6},{6,7},{8,9},{9,10},{10,11},{11... | collective-permute-start | bytes 99848 | tf_op jit(solution)/shard_map/ppermute | solution.py:22
  39.4 8.4 %collective-permute-start.6 = (f32[64,1,130]{2,1,0:T(1,128)S(1)}, f32[64,1,130]{2,1,0:T(1,128)S(1)}, u32[]{:S(2)}, u32[]{:S(2)}) collective-permute-start(f32[64,1,130]{2,1,0:T(1,128)S(1)} %get-tuple-element.304), channel_id=1, source_target_pairs={{1,0},{2,1},{3,2},{4,3},{5,4},{6,5},{7,6},{9,8},{10,9},{11,10},{12... | collective-permute-start | bytes 99848 | tf_op jit(solution)/shard_map/ppermute | solution.py:25
  42.2 6.2 collective-permute-start.5
  45.8 6.3 collective-permute-start.7
  53.2 1.1 copy-start.13
  53.3 1.1 copy-start.14
  54.3 4.8 copy-start.20
  54.4 5.6 copy-start.16
  54.7 12.2 %collective-permute-start.8 = (f32[2,64,8,1]{3,2,1,0:T(8,128)S(1)}, f32[2,64,8,1]{3,2,1,0:T(8,128)S(1)}, u32[]{:S(2)}, u32[]{:S(2)}) collective-permute-start(f32[2,64,8,1]{3,2,1,0:T(8,128)S(1)} %get-tuple-element.310), channel_id=1, source_target_pairs={{0,8},{8,16},{16,24},{24,32},{32,40},{40,48},{48,56},{56,64},{64,7... | collective-permute-start | bytes 12296 | tf_op jit(solution)/shard_map/ppermute | solution.py:22
  57.8 13.3 %collective-permute-start.9 = (f32[2,64,8,1]{3,2,1,0:T(8,128)S(1)}, f32[2,64,8,1]{3,2,1,0:T(8,128)S(1)}, u32[]{:S(2)}, u32[]{:S(2)}) collective-permute-start(f32[2,64,8,1]{3,2,1,0:T(8,128)S(1)} %get-tuple-element.311), channel_id=1, source_target_pairs={{8,0},{16,8},{24,16},{32,24},{40,32},{48,40},{56,48},{64,56},{72,6... | collective-permute-start | bytes 12296 | tf_op jit(solution)/shard_map/ppermute | solution.py:25
  59.2 0.8 copy-start
  60.0 24.3 %copy-start.10 = (f32[1,4096]{1,0:T(1,128)}, f32[1,4096]{1,0:T(1,128)S(1)}, u32[]{:S(2)}) copy-start(f32[1,4096]{1,0:T(1,128)S(1)} %slice.317) | copy-start | bytes 49156
  71.9 7.8 %collective-permute-start.10 = (f32[2,64,1,130]{3,2,1,0:T(1,128)S(1)}, f32[2,64,1,130]{3,2,1,0:T(1,128)S(1)}, u32[]{:S(2)}, u32[]{:S(2)}) collective-permute-start(f32[2,64,1,130]{3,2,1,0:T(1,128)S(1)} %get-tuple-element.295), channel_id=1, source_target_pairs={{0,1},{1,2},{2,3},{3,4},{4,5},{5,6},{6,7},{8,9},{9,10},{10,11},{11... | collective-permute-start | bytes 199688 | tf_op jit(solution)/shard_map/ppermute | solution.py:22
  77.0 6.3 collective-permute-start.11
  85.5 261.4 %copy-start.5 = (f32[2,64,8,128]{3,2,1,0:T(8,128)}, f32[2,64,8,128]{3,2,1,0:T(8,128)S(1)}, u32[]{:S(2)}) copy-start(f32[2,64,8,128]{3,2,1,0:T(8,128)S(1)} %pad_subtract_fusion) | copy-start | bytes 1572868
  346.8 260.7 %copy-start.7 = (f32[512,128]{1,0:T(8,128)S(1)}, f32[512,128]{1,0:T(8,128)}, u32[]{:S(2)}) copy-start(f32[512,128]{1,0:T(8,128)} %param.33) | copy-start | bytes 786436
  607.7 0.8 copy-start.22
  623.4 10.0 %copy-start.12 = (f32[1,4096]{1,0:T(1,128)S(1)}, f32[1,4096]{1,0:T(1,128)}, u32[]{:S(2)}) copy-start(f32[1,4096]{1,0:T(1,128)} %slice_add_fusion.2) | copy-start | bytes 49156
  623.4 11.6 %copy-start.1 = (f32[40,4096]{1,0:T(8,128)S(1)}, f32[40,4096]{1,0:T(8,128)}, u32[]{:S(2)}) copy-start(f32[40,4096]{1,0:T(8,128)} %copy-done) | copy-start | bytes 1966084
  623.4 34.8 %all-to-all-start.1 = ((f32[128,8,3,128]{3,1,2,0:T(8,128)}), f32[128,8,3,128]{3,1,2,0:T(8,128)S(1)}, u32[]{:S(2)}, u32[]{:S(2)}) async-start(f32[128,8,3,128]{3,1,2,0:T(8,128)} %copy.33), calls=%async_computation.1 | async-start | bytes 3145728 | tf_op jit(solution)/shard_map/all_to_all | solution.py:174
  633.3 4.9 copy-start.6
  633.3 4.9 copy-start.18
  633.3 4.9 copy-start.19
  658.6 0.9 copy-start.17
  658.6 4.1 copy-start.4
  658.7 4.1 copy-start.11
  755.0 0.8 copy-start.9
where the time goes:
time: 757 us; the launch traced here: 756 us
  local copies, waits for them, and re-layouts  637 us (84%)
  starting transfers between devices  57.8 us (8%)
  waiting for transfers between devices  37.4 us (5%)
  other arithmetic  17.7 us (2%)
    gather x1, local copies, waits for them, and re-layouts, local(): mean_base[pair_column]  261 us
    gather x1, local copies, waits for them, and re-layouts, local(): mean_melt[pair_column]  261 us
    dynamic_update_slice x120, local copies, waits for them, and re-layouts, solve_columns(): lax.scan(forward, start, (diagonal, below, above, right_side))  47.2 us
    dynamic_slice x120, local copies, waits for them, and re-layouts, solve_columns(): lax.scan(forward, start, (diagonal, below, above, right_side))  40 us
    ppermute x6, starting transfers between devices, padded(): lax.ppermute(lax.slice_in_dim(block, block.shape[dim] - width, None, axis...  23.5 us
    all_to_all x1, waiting for transfers between devices, local(): lax.all_to_all(send_values.reshape(devices, capacity, 3, block_width), ('...  19.1 us
  transfers between devices with their start and end apart: 14, of which 5 were waited for; matrix products, arithmetic and copies ran while one was open for 74% of the time, Pallas kernels for 0%

commit v1 on v0

v1 whole, which is shorter than its diff:
```python
import jax
import jax.numpy as jnp
from jax import lax
from jax.experimental import pallas as pl
from jax.experimental.pallas import tpu as pltpu
from jax.sharding import PartitionSpec as P

mixing_rate = 0.2
liquidus_slope = -0.0573
liquidus_base = 0.0832
liquidus_depth = -0.000753
latent_ratio = 4.0
salt_ratio = 35.0
relax_rate = 0.1
cold_rate = 2.0
temperate_rate = 0.2

f32 = jnp.float32
bf16 = jnp.bfloat16
levels = 64
slots = 8
chunk = 3 * slots + 1
halo_rows = 392


def lanes_of(shape):
    return lax.broadcasted_iota(jnp.int32, shape, len(shape) - 1)


def call(body, outs, ins, in_specs=None, scratch=(), cost=(0, 0)):
    return pl.pallas_call(
        body,
        out_shape=outs,
        grid=(1,),
        in_specs=in_specs,
        out_specs=jax.tree.map(lambda o: whole(o.shape), outs),
        scratch_shapes=scratch,
        cost_estimate=pl.CostEstimate(flops=cost[0], bytes_accessed=cost[1], transcendentals=0),
    )(*ins)


def whole(shape):
    return pl.BlockSpec(tuple(shape), lambda i: (0,) * len(shape))


def part(shape, *index):
    return pl.BlockSpec(tuple(shape), lambda i: index)


def row_pack_body(temp, salt, wet, mix, friction, pressure, up, down):
    for k in range(levels):
        for field, source in enumerate((temp, salt, wet)):
            at = 2 * (field * levels + k)
            up[at : at + 2, :] = source[k, 0:2, :].astype(f32)
            down[at : at + 2, :] = source[k, 6:8, :].astype(f32)
    for place, source in enumerate((mix, friction, pressure)):
        at = 2 * (3 * levels + place)
        up[at : at + 2, :] = source[0:2, :]
        down[at : at + 2, :] = source[6:8, :]
    up[390:392, :] = jnp.zeros((2, 128), f32)
    down[390:392, :] = jnp.zeros((2, 128), f32)


def col_pack_body(temp, salt, wet, mix, friction, pressure, top, bottom, left, right, tall):
    zeros = jnp.zeros((8, 128), f32)
    half = lanes_of((16, 128)) // 2

    def plane(at, centre):
        tall[at, 0:8, :] = centre
        tall[at, 8:16, :] = zeros
        tall[at, 8:10, :] = bottom[2 * at : 2 * at + 2, :]
        tall[at, 14:16, :] = top[2 * at : 2 * at + 2, :]

    for field, source in enumerate((temp, salt, wet)):
        for k in range(levels):
            plane(field * levels + k, source[k].astype(f32))
    for place, source in enumerate((mix, friction, pressure)):
        plane(3 * levels + place, source[...])
    for group in range(4):
        count = levels if group < 3 else 3
        go_left = jnp.zeros((16, 128), f32)
        go_right = jnp.zeros((16, 128), f32)
        for k in range(count):
            value = tall[group * levels + k]
            here = half == k
            go_left = jnp.where(here, pltpu.roll(value, 2 * k, 1), go_left)
            go_right = jnp.where(here, pltpu.roll(value, (2 * k + 2) % 128, 1), go_right)
        left[16 * group : 16 * group + 16, :] = go_left
        right[16 * group : 16 * group + 16, :] = go_right


def sides_of(from_right, from_left, back, ahead):
    lane = lanes_of((16, 128))
    return jnp.where(
        lane < 64, pltpu.roll(from_right, back, 1), pltpu.roll(from_left, ahead, 1)
    )


def dry_gap(side):
    lane = lanes_of((16, 128))
    return jnp.where((lane < 2) | (lane >= 126), side, 0.0)


def beside(value):
    rows, cols = value.shape
    return (
        pltpu.roll(value, 1, 0),
        pltpu.roll(value, rows - 1, 0),
        pltpu.roll(value, 1, 1),
        pltpu.roll(value, cols - 1, 1),
    )


def spread(value, links):
    change = jnp.zeros_like(value)
    for link, near in zip(links, beside(value)):
        change = change + link * (near - value)
    return value + mixing_rate * change


def links_of(wet):
    return tuple(wet * near for near in beside(wet))


def shelf_melt(surface_temp, surface_salt, friction, pressure, wet_top):
    heat_gain = jnp.where(wet_top > 0, friction, 1.0)
    salt_safe = jnp.where(wet_top > 0, surface_salt, 34.0)
    salt_gain = heat_gain / salt_ratio
    curvature = heat_gain * liquidus_slope
    linear = (
        heat_gain * (surface_temp - liquidus_base - liquidus_depth * pressure)
        + latent_ratio * salt_gain
    )
    constant = latent_ratio * salt_gain * salt_safe
    boundary_salt = (
        2.0 * constant / (linear + jnp.sqrt(linear * linear - 4.0 * curvature * constant))
    )
    boundary_temp = liquidus_slope * boundary_salt + liquidus_base + liquidus_depth * pressure
    heat_flux = heat_gain * (surface_temp - boundary_temp) * wet_top
    salt_flux = salt_gain * (salt_safe - boundary_salt) * wet_top
    return heat_flux, salt_flux, boundary_temp * wet_top


def centre_of(value):
    return value[0:8, 0:128]


def surface_body(
    temp,
    salt,
    wet,
    mix,
    friction,
    pressure,
    top_temp,
    top_salt,
    top_wet,
    top_rest,
    low_temp,
    low_salt,
    low_wet,
    low_rest,
    from_right,
    from_left,
    slot_row,
    slot_lane,
    slot_weight,
    slot_target,
    send,
    tall,
):
    def plane(at, group, k, centre, top, bottom, offset):
        tall[at, 0:8, 0:128] = centre
        tall[at, 8:16, 0:128] = jnp.zeros((8, 128), f32)
        tall[at, 8:10, 0:128] = bottom[offset : offset + 2, :]
        tall[at, 14:16, 0:128] = top[offset : offset + 2, :]
        side = sides_of(
            from_right[16 * group : 16 * group + 16, :],
            from_left[16 * group : 16 * group + 16, :],
            (128 - 2 * k) % 128,
            126 - 2 * k,
        )
        tall[at, :, 128:256] = dry_gap(side) if group == 2 else side

    for k in range(3):
        plane(k, 0, k, temp[k], top_temp, low_temp, 2 * k)
        plane(3 + k, 1, k, salt[k], top_salt, low_salt, 2 * k)
        plane(6 + k, 2, k, wet[k].astype(f32), top_wet, low_wet, 2 * k)
    for place, (source) in enumerate((mix, friction, pressure)):
        plane(9 + place, 3, place, source[...], top_rest, low_rest, 2 * place)

    wets = [tall[6 + k] for k in range(3)]
    mixing = tall[9]
    rub = tall[10]
    press = tall[11]
    first = mixing * (wets[0] * wets[1])
    second = mixing * (wets[1] * wets[2])
    links = [links_of(value) for value in wets]
    stepped = []
    for field in range(2):
        near = [spread(tall[3 * field + k], links[k]) for k in range(3)]
        flux = first * (near[1] - near[0])
        under = second * (near[2] - near[1])
        stepped.append((near[0] + flux, near[1] + under - flux))
    heat, brine, base_one = shelf_melt(stepped[0][0], stepped[1][0], rub, press, wets[0])
    tops = (stepped[0][0] - relax_rate * heat, stepped[1][0] - relax_rate * brine)
    later = []
    for field in range(2):
        near0 = spread(tops[field], links[0])
        near1 = spread(stepped[field][1], links[1])
        later.append(centre_of(near0 + first * (near1 - near0)))
    heat_two, unused, base_two = shelf_melt(
        later[0], later[1], friction[...], pressure[...], centre_of(wets[0])
    )
    melt = 0.5 * (centre_of(heat) / latent_ratio + heat_two / latent_ratio)
    base = 0.5 * (centre_of(base_one) + base_two)

    melts = [jnp.broadcast_to(melt[r : r + 1, :], (8, 128)) for r in range(8)]
    bases = [jnp.broadcast_to(base[r : r + 1, :], (8, 128)) for r in range(8)]

    def owners(i, carry):
        out = send.at[pl.ds(pl.multiple_of(8 * chunk * i, 8), 8 * chunk)]
        for j in range(8):
            at = pl.ds(pl.multiple_of(64 * i + 8 * j, 8), 8)
            lane = slot_lane[at, :]
            row = slot_row[at, :]
            weight = slot_weight[at, :]
            melt_here = jnp.take_along_axis(melts[0], lane, axis=1)
            base_here = jnp.take_along_axis(bases[0], lane, axis=1)
            for r in range(1, 8):
                hit = row == r
                melt_here = jnp.where(
                    hit, jnp.take_along_axis(melts[r], lane, axis=1), melt_here
                )
                base_here = jnp.where(
                    hit, jnp.take_along_axis(bases[r], lane, axis=1), base_here
                )
            out[chunk * j : chunk * j + 8, :] = weight * melt_here
            out[chunk * j + 8 : chunk * j + 16, :] = weight * base_here
            out[chunk * j + 16 : chunk * j + 24, :] = weight
        targets = slot_target[pl.ds(pl.multiple_of(8 * i, 8), 8), :]
        for j in range(8):
            out[chunk * j + 24 : chunk * j + 25, :] = targets[j : j + 1, :]
        return carry

    lax.fori_loop(0, 16, owners, 0)


def slot_body(owner, target, column, weight, slot_row, slot_lane, slot_weight, slot_target):
    count = owner.shape[0]
    across = jnp.broadcast_to(owner[...], (count, count))
    row = lax.broadcasted_iota(jnp.int32, (count, count), 0)
    col = lax.broadcasted_iota(jnp.int32, (count, count), 1)
    same = row == col
    owner_lane = jnp.sum(jnp.where(same, across, 0), axis=0, keepdims=True)
    alike = across == owner_lane
    rank_lane = jnp.sum(jnp.where(alike & (row < col), 1, 0), axis=0, keepdims=True)
    rank_row = jnp.sum(jnp.where(alike & (col < row), 1, 0), axis=1, keepdims=True)
    target_row = jnp.sum(jnp.where(same, target[...], 0), axis=1, keepdims=True)
    slot = owner_lane * slots + rank_lane
    total = slot_row.shape[0]
    pick = jnp.where(lax.broadcasted_iota(jnp.int32, (total, count), 0) == slot, 1.0, 0.0)
    value = weight[...]
    high = value.astype(bf16)
    rest = value - high.astype(f32)
    middle = rest.astype(bf16)
    low = (rest - middle.astype(f32)).astype(bf16)
    places = column[...]
    table = jnp.concatenate(
        [
            high,
            middle,
            low,
            (places // 128).astype(f32).astype(bf16),
            (places % 128).astype(f32).astype(bf16),
        ],
        axis=1,
    )
    sorted_ = jnp.dot(pick.astype(bf16), table, preferred_element_type=f32)
    slot_weight[...] = sorted_[:, 0:128] + sorted_[:, 128:256] + sorted_[:, 256:384]
    slot_row[...] = sorted_[:, 384:512].astype(jnp.int32)
    slot_lane[...] = sorted_[:, 512:640].astype(jnp.int32)
    lane = lax.broadcasted_iota(jnp.int32, (count, 128), 1)
    spot = jnp.where(rank_row == lane % slots, target_row, 0).astype(f32).astype(bf16)
    holds = jnp.where(lax.broadcasted_iota(jnp.int32, (128, count), 0) == owner_lane, 1.0, 0.0)
    slot_target[...] = jnp.dot(holds.astype(bf16), spot, preferred_element_type=f32)


def ocean_body(
    temp,
    salt,
    wet,
    mix,
    friction,
    pressure,
    top,
    bottom,
    from_right,
    from_left,
    new_temp,
    new_salt,
    tall,
    above,
):
    zeros = jnp.zeros((8, 128), f32)

    def rest_plane(at, source):
        tall[at, 0:8, 0:128] = source[...]
        tall[at, 8:16, 0:128] = zeros
        tall[at, 8:10, 0:128] = bottom[384 + 2 * at : 386 + 2 * at, :]
        tall[at, 14:16, 0:128] = top[384 + 2 * at : 386 + 2 * at, :]
        tall[at, :, 128:256] = sides_of(
            from_right[48:64, :], from_left[48:64, :], (128 - 2 * at) % 128, 126 - 2 * at
        )

    for at, source in enumerate((mix, friction, pressure)):
        rest_plane(at, source)
    mixing = tall[0]

    def build(spot, group, k, centre):
        offset = 2 * (group * levels + k)
        tall[spot, 0:8, 0:128] = centre
        tall[spot, 8:16, 0:128] = zeros
        tall[spot, 8:10, 0:128] = bottom[pl.ds(offset, 2), :]
        tall[spot, 14:16, 0:128] = top[pl.ds(offset, 2), :]
        side = sides_of(
            from_right[16 * group : 16 * group + 16, :],
            from_left[16 * group : 16 * group + 16, :],
            lax.rem(128 - 2 * k, 128),
            126 - 2 * k,
        )
        tall[spot, :, 128:256] = dry_gap(side) if group == 2 else side

    def load(k):
        build(3, 0, k, temp[k])
        build(4, 1, k, salt[k])
        build(5, 2, k, wet[k].astype(f32))
        water = tall[5]
        links = links_of(water)
        near = tuple(spread(tall[3 + field], links) for field in range(2))
        return water, links, near

    def second_step(k, once, water, links, state):
        middle_links = tuple(centre_of(link) for link in links)
        here = []
        for field in range(2):
            change = jnp.zeros((8, 128), f32)
            middle = centre_of(once[field])
            for link, near in zip(middle_links, beside(once[field])):
                change = change + link * (centre_of(near) - middle)
            here.append(middle + mixing_rate * change)
        water_c = centre_of(water)
        return tuple(here), water_c

    def emit(k, field, value):
        (new_temp, new_salt)[field][k] = value

    water0, links0, near0 = load(0)
    water1, links1, near1 = load(1)
    coef = mixing * (water0 * water1)
    flux = tuple(coef * (near1[f] - near0[f]) for f in range(2))
    first = tuple(near0[f] + flux[f] for f in range(2))
    heat, brine, unused = shelf_melt(first[0], first[1], tall[1], tall[2], water0)
    first = (first[0] - relax_rate * heat, first[1] - relax_rate * brine)
    here, water_c = second_step(0, first, water0, links0, None)
    mixing_c = mix[...]
    no_flux = (jnp.zeros((8, 128), f32), jnp.zeros((8, 128), f32))

    def finish(k, here, next_here, water_c, next_water, flux_c):
        coef_c = mixing_c * (water_c * next_water)
        out_flux = tuple(coef_c * (next_here[f] - here[f]) for f in range(2))
        return out_flux

    def advance(k, carry):
        water, links, near, flux, here, water_c, flux_c = carry
        next_water, next_links, next_near = load(k + 1)
        coef = mixing * (water * next_water)
        next_flux = tuple(coef * (next_near[f] - near[f]) for f in range(2))
        once = tuple(near[f] + next_flux[f] - flux[f] for f in range(2))
        next_here, next_c = second_step(k, once, water, links, None)
        out_flux = finish(k - 1, here, next_here, water_c, next_c, flux_c)
        for f in range(2):
            above[f, k - 1] = here[f] + out_flux[f] - flux_c[f]
        return next_water, next_links, next_near, next_flux, next_here, next_c, out_flux

    carry = (water1, links1, near1, flux, here, water_c, no_flux)
    carry = lax.fori_loop(1, levels - 1, advance, carry)
    water, links, near, flux, here, water_c, flux_c = carry
    once = tuple(near[f] - flux[f] for f in range(2))
    next_here, next_c = second_step(levels - 1, once, water, links, None)
    out_flux = finish(levels - 2, here, next_here, water_c, next_c, flux_c)
    for f in range(2):
        above[f, levels - 2] = here[f] + out_flux[f] - flux_c[f]
        above[f, levels - 1] = next_here[f] - out_flux[f]
    heat, brine, unused = shelf_melt(
        above[0, 0], above[1, 0], friction[...], pressure[...], wet[0].astype(f32)
    )
    above[0, 0] = above[0, 0] - relax_rate * heat
    above[1, 0] = above[1, 0] - relax_rate * brine
    new_temp[...] = above[0]
    new_salt[...] = above[1]


def column_body(enthalpy, surface, transition, offset, factor, pivot_end, side_end):
    count = enthalpy.shape[0]
    side = enthalpy[...].reshape(count, 32, 128)
    change_at = transition[...]
    rates = [jnp.where(k < change_at, cold_rate, temperate_rate) for k in range(count)]
    inner = [0.5 * (rates[k] + rates[k + 1]) for k in range(count - 1)]
    ratios = []
    values = []
    for k in range(count - 1):
        if k == 0:
            pivot = 1.0 + rates[0] + inner[0]
            right = side[0] + rates[0] * surface[...]
        else:
            pivot = 1.0 + inner[k - 1] + inner[k] + inner[k - 1] * ratios[-1]
            right = side[k] + inner[k - 1] * values[-1]
        scale = 1.0 / pivot
        ratios.append(-inner[k] * scale)
        values.append(right * scale)
    pivot_end[...] = 1.0 + inner[-1] + inner[-1] * ratios[-1]
    side_end[...] = side[count - 1] + inner[-1] * values[-1]
    offsets = [jnp.zeros((32, 128), f32)]
    factors = [jnp.ones((32, 128), f32)]
    for k in range(count - 2, -1, -1):
        offsets.append(values[k] - ratios[k] * offsets[-1])
        factors.append(-ratios[k] * factors[-1])
    offset[...] = jnp.stack(offsets[::-1]).reshape(count, 4096)
    factor[...] = jnp.stack(factors[::-1]).reshape(count, 4096)


def collect_body(got, area, offset, factor, pivot_end, side_end, new_enthalpy, melt):
    sums = jnp.zeros((32, 384), f32)
    lane = lax.broadcasted_iota(jnp.int32, (1, 128), 1) // slots
    wanted = lax.broadcasted_iota(jnp.int32, (32, 128), 0).astype(f32)
    for group in range(8):
        parts = ([], [], [])
        target = jnp.zeros((1, 128), f32)
        for s in range(16):
            at = chunk * (16 * group + s)
            for place in range(3):
                parts[place].append(got[at + 8 * place : at + 8 * place + 8, :])
            target = jnp.where(lane == s, got[at + 24 : at + 25, :], target)
        hot = jnp.where(wanted == target, 1.0, 0.0).astype(bf16)
        value = jnp.concatenate([jnp.concatenate(p, axis=0) for p in parts], axis=1)
        high = value.astype(bf16)
        rest = value - high.astype(f32)
        middle = rest.astype(bf16)
        low = (rest - middle.astype(f32)).astype(bf16)
        for piece in (high, middle, low):
            sums = sums + jnp.dot(hot, piece, preferred_element_type=f32)
    size = area[...]
    melt[...] = sums[:, 0:128] / size
    base_sum = sums[:, 128:256] / size
    cover_sum = sums[:, 256:384] / size
    last = (side_end[...] + base_sum) / (pivot_end[...] + cover_sum)
    last = last.reshape(1, 4096)
    new_enthalpy[...] = offset[...] + factor[...] * last


def local(
    ocean_temp,
    ocean_salt,
    wet_mask,
    vertical_mix,
    friction,
    pressure,
    pair_column,
    pair_weight,
    block_owner,
    block_target,
    enthalpy,
    surface_enthalpy,
    transition_layer,
    column_area,
):
    shape = jax.ShapeDtypeStruct
    ocean = (ocean_temp, ocean_salt, wet_mask, vertical_mix, friction, pressure)
    ocean_specs = [whole(a.shape) for a in ocean]
    count_x = lax.axis_size("gx")
    count_y = lax.axis_size("gy")
    ahead = lambda n: [(i, i + 1) for i in range(n - 1)]
    back = lambda n: [(i + 1, i) for i in range(n - 1)]
    rows_shape = shape((halo_rows, 128), f32)
    up, down = call(
        row_pack_body, (rows_shape, rows_shape), ocean, ocean_specs, cost=(10**5, 10**6)
    )
    bottom = lax.ppermute(up, "gy", back(count_y))
    top = lax.ppermute(down, "gy", ahead(count_y))
    slots_shape = count_x * count_y * slots
    slot_ins = (block_owner, block_target.reshape(1, -1), pair_column, pair_weight)
    slot_row, slot_lane, slot_weight, slot_target = call(
        slot_body,
        (
            shape((slots_shape, 128), jnp.int32),
            shape((slots_shape, 128), jnp.int32),
            shape((slots_shape, 128), f32),
            shape((count_x * count_y, 128), f32),
        ),
        slot_ins,
        [whole(a.shape) for a in slot_ins],
        cost=(2 * 10**9, 3 * 10**6),
    )
    cols_shape = shape((64, 128), f32)
    left, right = call(
        col_pack_body,
        (cols_shape, cols_shape),
        ocean + (top, bottom),
        ocean_specs + [whole((halo_rows, 128))] * 2,
        [pltpu.VMEM((3 * levels + 3, 16, 128), f32)],
        cost=(10**5, 10**6),
    )
    from_right = lax.ppermute(left, "gx", back(count_x))
    from_left = lax.ppermute(right, "gx", ahead(count_x))
    tile = (8, 128)
    few = (4, 8, 128)
    send = call(
        surface_body,
        shape((count_x * count_y * chunk, 128), f32),
        ocean
        + (top,) * 4
        + (bottom,) * 4
        + (from_right, from_left, slot_row, slot_lane, slot_weight, slot_target),
        [part(few, 0, 0, 0)] * 3
        + [part(tile, 0, 0)] * 3
        + [part(tile, b, 0) for b in (0, 16, 32, 48)] * 2
        + [whole((64, 128))] * 2
        + [whole((slots_shape, 128))] * 3
        + [whole((count_x * count_y, 128))],
        [pltpu.VMEM((12, 16, 256), f32)],
        cost=(10**6, 3 * 10**6),
    )
    send, bottom, surface_enthalpy = lax.optimization_barrier((send, bottom, surface_enthalpy))
    got = lax.all_to_all(
        send.reshape(count_x * count_y, chunk, 1, 128),
        ("gx", "gy"),
        split_axis=0,
        concat_axis=0,
        tiled=True,
    ).reshape(count_x * count_y * chunk, 128)
    new_temp, new_salt = call(
        ocean_body,
        (shape(ocean_temp.shape, f32), shape(ocean_salt.shape, f32)),
        ocean + (top, bottom, from_right, from_left),
        ocean_specs + [whole((halo_rows, 128))] * 2 + [whole((64, 128))] * 2,
        [pltpu.VMEM((6, 16, 256), f32), pltpu.VMEM((2, levels, 8, 128), f32)],
        cost=(10**8, 2 * 10**6),
    )
    ice_shape = shape((32, 128), f32)
    column_ins = (enthalpy, surface_enthalpy.reshape(32, 128), transition_layer.reshape(32, 128))
    offset, factor, pivot_end, side_end = call(
        column_body,
        (shape(enthalpy.shape, f32), shape(enthalpy.shape, f32), ice_shape, ice_shape),
        column_ins,
        [whole(a.shape) for a in column_ins],
        cost=(10**8, 2 * 10**6),
    )
    last_ins = (got, column_area.reshape(32, 128), offset, factor, pivot_end, side_end)
    new_enthalpy, melt = call(
        collect_body,
        (shape(enthalpy.shape, f32), ice_shape),
        last_ins,
        [whole(a.shape) for a in last_ins],
        cost=(10**9, 4 * 10**6),
    )
    return new_temp, new_salt, new_enthalpy, melt.reshape(-1)


def solution(mesh):
    return jax.shard_map(
        local,
        mesh=mesh,
        in_specs=(
            P(None, "gy", "gx"),
            P(None, "gy", "gx"),
            P(None, "gy", "gx"),
            P("gy", "gx"),
            P("gy", "gx"),
            P("gy", "gx"),
            P(("gx", "gy"), None),
            P(("gx", "gy"), None),
            P(("gx", "gy"), None),
            P(("gx", "gy")),
            P(None, ("gx", "gy")),
            P(("gx", "gy")),
            P(("gx", "gy")),
            P(("gx", "gy")),
        ),
        out_specs=(
            P(None, "gy", "gx"),
            P(None, "gy", "gx"),
            P(None, ("gx", "gy")),
            P(("gx", "gy")),
        ),
        check_vma=False,
    )
```

time: 757 us -> 76.4 us (0.10)
  local copies, waits for them, and re-layouts: 637 us -> 4.03 us
  Pallas kernels: 0 us -> 39.3 us
  starting transfers between devices: 57.8 us -> 23.3 us
  waiting for transfers between devices: 37.4 us -> 8.68 us
  other arithmetic: 17.7 us -> 0 us
    gather x2 -> x0, local copies, waits for them, and re-layouts: 521 us -> none  [the longest x1 261 us: local(): mean_base[pair_column]]
    dynamic_update_slice x120 -> x0, local copies, waits for them, and re-layouts: 47.2 us -> none  [solve_columns(): lax.scan(forward, start, (diagonal, below, above, right_side))]
    dynamic_slice x120 -> x0, local copies, waits for them, and re-layouts: 40 us -> none  [solve_columns(): lax.scan(forward, start, (diagonal, below, above, right_side))]
    pallas_call x0 -> x7, Pallas kernels: none -> 39.3 us  [call(): pl.pallas_call(body, out_shape=outs, grid=(1,), in_specs=in_specs, out_sp...]
    ppermute x12 -> x4, starting transfers between devices: 33.3 us -> 11.7 us  [the longest x1 4.49 us: local(): top = lax.ppermute(down, 'gy', ahead(count_y))]
    scatter x2 -> x0, local copies, waits for them, and re-layouts: 16 us -> none  [the longest x1 13.6 us: local(): jnp.zeros((devices * capacity, 3, block_width), jnp.float32).at[slot]]
    ppermute x12 -> x4, waiting for transfers between devices: 18.3 us -> 3.78 us  [the longest x1 3.77 us: local(): bottom = lax.ppermute(up, 'gy', back(count_y))]
    all_to_all x2 -> x1, waiting for transfers between devices: 19.1 us -> 4.9 us  [local(): lax.all_to_all(send.reshape(count_x * count_y, chunk, 1, 128), ('gx', 'gy...]
  transfers between devices with their start and end apart: 14 -> 5, of which waited for: 5 -> 2; matrix products, arithmetic and copies ran while one was open for 74% -> 2% of each run, Pallas kernels for 0% -> 32%
where the time goes in v1:
time: 76.4 us; the launch traced here: 75.9 us
  Pallas kernels  39.3 us (51%)
  starting transfers between devices  23.3 us (30%)
  waiting for transfers between devices  8.68 us (11%)
  local copies, waits for them, and re-layouts  4.03 us (5%)
    pallas_call x7, Pallas kernels, call(): pl.pallas_call(body, out_shape=outs, grid=(1,), in_specs=in_specs, out_sp...  39.3 us
    all_to_all x1, starting transfers between devices, local(): lax.all_to_all(send.reshape(count_x * count_y, chunk, 1, 128), ('gx', 'gy...  11.6 us
    all_to_all x1, waiting for transfers between devices, local(): lax.all_to_all(send.reshape(count_x * count_y, chunk, 1, 128), ('gx', 'gy...  4.9 us
    ppermute x1, starting transfers between devices, local(): top = lax.ppermute(down, 'gy', ahead(count_y))  4.49 us
    unnamed x11, local copies, waits for them, and re-layouts  4.03 us
    ppermute x1, starting transfers between devices, local(): from_left = lax.ppermute(right, 'gx', ahead(count_x))  3.99 us
    ppermute x1, waiting for transfers between devices, local(): bottom = lax.ppermute(up, 'gy', back(count_y))  3.77 us
    ppermute x1, starting transfers between devices, local(): bottom = lax.ppermute(up, 'gy', back(count_y))  1.92 us
  transfers between devices with their start and end apart: 5, of which 2 were waited for; matrix products, arithmetic and copies ran while one was open for 2% of the time, Pallas kernels for 32%

profile of v1, /device:TPU:1, one launch (start us, length us, event | category | flops | bytes accessed | tf_op | source)
XLA Modules:
  0.0 75.9 jit_solution(12086040691735362398)
XLA Ops:
  0.6 2.0 %shard_map.165 = (f32[392,128]{1,0:T(8,128)}, f32[392,128]{1,0:T(8,128)}) custom-call(f32[64,8,128]{2,1,0:T(8,128)} %temp.7, f32[64,8,128]{2,1,0:T(8,128)} %salt.7, s32[64,8,128]{2,1,0:T(8,128)} %wet.7, f32[8,128]{1,0:T(8,128)} %mix.7, f32[8,128]{1,0:T(8,128)} %friction.7, f32[8,128]{1,0:T(8,128)} %pressure.7), custom_call_target="tpu_custom_call" | custom-call | flops 100000 | bytes 1000000 | tf_op jit(solution)/shard_map/pallas_call | solution.py:31
  2.6 4.5 %collective-permute-start = (f32[392,128]{1,0:T(8,128)}, f32[392,128]{1,0:T(8,128)S(1)}, u32[]{:S(2)}, u32[]{:S(2)}) collective-permute-start(f32[392,128]{1,0:T(8,128)} %get-tuple-element.23), channel_id=1, source_target_pairs={{0,1},{1,2},{2,3},{3,4},{4,5},{5,6},{6,7},{8,9},{9,10},{10,11},{11... | collective-permute-start | bytes 602120 | tf_op jit(solution)/shard_map/ppermute | solution.py:490
  7.1 1.9 %collective-permute-start.1 = (f32[392,128]{1,0:T(8,128)}, f32[392,128]{1,0:T(8,128)S(1)}, u32[]{:S(2)}, u32[]{:S(2)}) collective-permute-start(f32[392,128]{1,0:T(8,128)} %get-tuple-element.24), channel_id=1, source_target_pairs={{1,0},{2,1},{3,2},{4,3},{5,4},{6,5},{7,6},{9,8},{10,9},{11,10},{12... | collective-permute-start | bytes 602120 | tf_op jit(solution)/shard_map/ppermute | solution.py:489
  9.1 1.5 %copy.20.owner = s32[512,1]{1,0:T(8,128)} copy(s32[512,1]{0,1:T(1,128)} %param.22) | data formatting | bytes 4096 | tf_op args[8]
  10.6 0.0 collective-permute-done.top.top_temp.top_salt.top_wet.top_rest
  10.6 0.0 copy-start
  10.6 3.8 %collective-permute-done.1.bottom.low_temp.low_salt.low_wet.low_rest = f32[392,128]{1,0:T(8,128)S(1)} collective-permute-done((f32[392,128]{1,0:T(8,128)}, f32[392,128]{1,0:T(8,128)S(1)}, u32[]{:S(2)}, u32[]{:S(2)}) %collective-permute-start.1) | collective-permute-done | bytes 200736 | tf_op jit(solution)/shard_map/ppermute | solution.py:489
  14.4 0.0 copy-done
  14.4 0.0 copy-start.1
  14.4 0.7 copy-done.1
  15.1 2.9 %shard_map.166 = (f32[64,128]{1,0:T(8,128)}, f32[64,128]{1,0:T(8,128)}) custom-call(f32[64,8,128]{2,1,0:T(8,128)} %temp.7, f32[64,8,128]{2,1,0:T(8,128)} %salt.7, s32[64,8,128]{2,1,0:T(8,128)} %wet.7, f32[8,128]{1,0:T(8,128)} %mix.7, f32[8,128]{1,0:T(8,128)} %friction.7, f32[8,128]{1,0:T(8,128)} %pressure.7, f32[392,128]{1,0:T(8,128)} %copy-done, ...), custom_call_target="tpu_custom_call" | custom-call | flops 100000 | bytes 1000000 | tf_op jit(solution)/shard_map/pallas_call | solution.py:31
  18.0 1.3 %collective-permute-start.2 = (f32[64,128]{1,0:T(8,128)}, f32[64,128]{1,0:T(8,128)S(1)}, u32[]{:S(2)}, u32[]{:S(2)}) collective-permute-start(f32[64,128]{1,0:T(8,128)} %get-tuple-element.25), channel_id=1, source_target_pairs={{8,0},{16,8},{24,16},{32,24},{40,32},{48,40},{56,48},{64,56},{72,6... | collective-permute-start | bytes 98312 | tf_op jit(solution)/shard_map/ppermute | solution.py:514
  19.2 4.0 %collective-permute-start.3 = (f32[64,128]{1,0:T(8,128)}, f32[64,128]{1,0:T(8,128)S(1)}, u32[]{:S(2)}, u32[]{:S(2)}) collective-permute-start(f32[64,128]{1,0:T(8,128)} %get-tuple-element.26), channel_id=1, source_target_pairs={{0,8},{8,16},{16,24},{24,32},{32,40},{40,48},{48,56},{56,64},{64,7... | collective-permute-start | bytes 98312 | tf_op jit(solution)/shard_map/ppermute | solution.py:515
  23.2 3.7 %shard_map.167 = (s32[1024,128]{1,0:T(8,128)}, s32[1024,128]{1,0:T(8,128)}, f32[1024,128]{1,0:T(8,128)}, f32[128,128]{1,0:T(8,128)}) custom-call(s32[512,1]{1,0:T(8,128)} %copy.20.owner, s32[1,512]{1,0:T(1,128)} %bitcast.12, s32[512,128]{1,0:T(8,128)} %column.1, f32[512,128]{1,0:T(8,128)} %weight.1), custom_call_target="tpu_custom_call" | custom-call | flops 2000000000 | bytes 3000000 | tf_op jit(solution)/shard_map/pallas_call | solution.py:31
  27.0 0.0 collective-permute-done.2.from_right
  27.0 0.0 copy-start.3
  27.0 0.0 collective-permute-done.3.from_left
  27.0 0.0 copy-start.4
  27.0 0.6 copy-done.3
  27.6 0.0 copy-done.4
  27.6 6.7 %shard_map.168 = f32[3200,128]{1,0:T(8,128)} custom-call(f32[64,8,128]{2,1,0:T(8,128)} %temp.7, f32[64,8,128]{2,1,0:T(8,128)} %salt.7, s32[64,8,128]{2,1,0:T(8,128)} %wet.7, f32[8,128]{1,0:T(8,128)} %mix.7, f32[8,128]{1,0:T(8,128)} %friction.7, f32[8,128]{1,0:T(8,128)} %pressure.7, f32[392,128]{1,0:T(8,128)} %copy-done, f32[392,128]{1,0:T(8,128)} %copy-done, ...), custom_call_target="tpu_custom_call" | custom-call | flops 1000000 | bytes 3000000 | tf_op jit(solution)/shard_map/pallas_call | solution.py:31
  34.3 11.6 %all-to-all-start = ((f32[128,25,1,128]{3,2,1,0:T(1,128)}), f32[128,25,1,128]{3,2,1,0:T(1,128)S(1)}, u32[]{:S(2)}, u32[]{:S(2)}) async-start(f32[128,25,1,128]{3,2,1,0:T(1,128)} %bitcast.7), calls=%async_computation | async-start | bytes 3276800 | tf_op jit(solution)/shard_map/all_to_all | solution.py:535
  45.9 2.8 %shard_map.170 = (f32[40,4096]{1,0:T(8,128)}, f32[40,4096]{1,0:T(8,128)}, f32[32,128]{1,0:T(8,128)}, f32[32,128]{1,0:T(8,128)}) custom-call(f32[40,4096]{1,0:T(8,128)} %enthalpy.1, f32[32,128]{1,0:T(8,128)} %bitcast.9, s32[32,128]{1,0:T(8,128)} %bitcast.10), custom_call_target="tpu_custom_call" | custom-call | flops 100000000 | bytes 2000000 | tf_op jit(solution)/shard_map/pallas_call | solution.py:31
  48.7 17.8 %shard_map.169 = (f32[64,8,128]{2,1,0:T(8,128)}, f32[64,8,128]{2,1,0:T(8,128)}) custom-call(f32[64,8,128]{2,1,0:T(8,128)} %temp.7, f32[64,8,128]{2,1,0:T(8,128)} %salt.7, s32[64,8,128]{2,1,0:T(8,128)} %wet.7, f32[8,128]{1,0:T(8,128)} %mix.7, f32[8,128]{1,0:T(8,128)} %friction.7, f32[8,128]{1,0:T(8,128)} %pressure.7, f32[392,128]{1,0:T(8,128)} %copy-done, ...), custom_call_target="tpu_custom_call" | custom-call | flops 100000000 | bytes 2000000 | tf_op jit(solution)/shard_map/pallas_call | solution.py:31
  66.6 4.9 %all-to-all-done = f32[128,25,1,128]{3,2,1,0:T(1,128)S(1)} async-done(((f32[128,25,1,128]{3,2,1,0:T(1,128)}), f32[128,25,1,128]{3,2,1,0:T(1,128)S(1)}, u32[]{:S(2)}, u32[]{:S(2)}) %all-to-all-start) | async-done | bytes 1638432 | tf_op jit(solution)/shard_map/all_to_all | solution.py:535
  71.5 0.0 copy-start.2
  71.5 1.2 %copy-done.2 = f32[128,25,1,128]{3,2,1,0:T(1,128)} copy-done((f32[128,25,1,128]{3,2,1,0:T(1,128)}, f32[128,25,1,128]{3,2,1,0:T(1,128)S(1)}, u32[]{:S(2)}) %copy-start.2) | copy-done | bytes 1638424
  72.7 3.3 %shard_map.171 = (f32[40,4096]{1,0:T(8,128)}, f32[32,128]{1,0:T(8,128)}) custom-call(f32[3200,128]{1,0:T(8,128)} %bitcast.8, f32[32,128]{1,0:T(8,128)} %bitcast.11, f32[40,4096]{1,0:T(8,128)} %get-tuple-element.36.offset, f32[40,4096]{1,0:T(8,128)} %get-tuple-element.37.factor, f32[32,128]{1,0:T(8,128)} %get-tuple-element.38.pivot_end, ...), custom_call_target="tpu_custom_call" | custom-call | flops 1000000000 | bytes 4000000 | tf_op jit(solution)/shard_map/pallas_call | solution.py:31
Async XLA Ops:
  2.6 8.0 %collective-permute-start = (f32[392,128]{1,0:T(8,128)}, f32[392,128]{1,0:T(8,128)S(1)}, u32[]{:S(2)}, u32[]{:S(2)}) collective-permute-start(f32[392,128]{1,0:T(8,128)} %get-tuple-element.23), channel_id=1, source_target_pairs={{0,1},{1,2},{2,3},{3,4},{4,5},{5,6},{6,7},{8,9},{9,10},{10,11},{11... | collective-permute-start | bytes 602120 | tf_op jit(solution)/shard_map/ppermute | solution.py:490
  7.1 7.2 %collective-permute-start.1 = (f32[392,128]{1,0:T(8,128)}, f32[392,128]{1,0:T(8,128)S(1)}, u32[]{:S(2)}, u32[]{:S(2)}) collective-permute-start(f32[392,128]{1,0:T(8,128)} %get-tuple-element.24), channel_id=1, source_target_pairs={{1,0},{2,1},{3,2},{4,3},{5,4},{6,5},{7,6},{9,8},{10,9},{11,10},{12... | collective-permute-start | bytes 602120 | tf_op jit(solution)/shard_map/ppermute | solution.py:489
  10.6 3.8 %copy-start = (f32[392,128]{1,0:T(8,128)}, f32[392,128]{1,0:T(8,128)S(1)}, u32[]{:S(2)}) copy-start(f32[392,128]{1,0:T(8,128)S(1)} %collective-permute-done.top.top_temp.top_salt.top_wet.top_rest) | copy-start | bytes 602116
  14.4 0.7 copy-start.1
  18.0 9.0 %collective-permute-start.2 = (f32[64,128]{1,0:T(8,128)}, f32[64,128]{1,0:T(8,128)S(1)}, u32[]{:S(2)}, u32[]{:S(2)}) collective-permute-start(f32[64,128]{1,0:T(8,128)} %get-tuple-element.25), channel_id=1, source_target_pairs={{8,0},{16,8},{24,16},{32,24},{40,32},{48,40},{56,48},{64,56},{72,6... | collective-permute-start | bytes 98312 | tf_op jit(solution)/shard_map/ppermute | solution.py:514
  19.2 7.7 %collective-permute-start.3 = (f32[64,128]{1,0:T(8,128)}, f32[64,128]{1,0:T(8,128)S(1)}, u32[]{:S(2)}, u32[]{:S(2)}) collective-permute-start(f32[64,128]{1,0:T(8,128)} %get-tuple-element.26), channel_id=1, source_target_pairs={{0,8},{8,16},{16,24},{24,32},{32,40},{40,48},{48,56},{56,64},{64,7... | collective-permute-start | bytes 98312 | tf_op jit(solution)/shard_map/ppermute | solution.py:515
  27.0 0.6 copy-start.3
  27.0 0.6 copy-start.4
  34.3 37.1 %all-to-all-start = ((f32[128,25,1,128]{3,2,1,0:T(1,128)}), f32[128,25,1,128]{3,2,1,0:T(1,128)S(1)}, u32[]{:S(2)}, u32[]{:S(2)}) async-start(f32[128,25,1,128]{3,2,1,0:T(1,128)} %bitcast.7), calls=%async_computation | async-start | bytes 3276800 | tf_op jit(solution)/shard_map/all_to_all | solution.py:535
  71.5 1.2 %copy-start.2 = (f32[128,25,1,128]{3,2,1,0:T(1,128)}, f32[128,25,1,128]{3,2,1,0:T(1,128)S(1)}, u32[]{:S(2)}) copy-start(f32[128,25,1,128]{3,2,1,0:T(1,128)S(1)} %all-to-all-done) | copy-start | bytes 4915204

commit v2 on v1

v2 whole, which is shorter than its diff:
```python
import jax
import jax.numpy as jnp
from jax import lax
from jax.experimental import pallas as pl
from jax.experimental.pallas import tpu as pltpu
from jax.sharding import PartitionSpec as P

mixing_rate = 0.2
liquidus_slope = -0.0573
liquidus_base = 0.0832
liquidus_depth = -0.000753
latent_ratio = 4.0
salt_ratio = 35.0
relax_rate = 0.1
cold_rate = 2.0
temperate_rate = 0.2

f32 = jnp.float32
bf16 = jnp.bfloat16
levels = 64
slots = 8
chunk = 3 * slots + 1
halo_rows = 392
few = 3


def lanes_of(shape):
    return lax.broadcasted_iota(jnp.int32, shape, len(shape) - 1)


def call(body, outs, ins, scratch=(), cost=(0, 0)):
    arrays, specs = [], []
    for item in ins:
        if isinstance(item, Near):
            arrays.append(pltpu.with_memory_space_constraint(item.array, pltpu.VMEM))
            specs.append(pl.BlockSpec(memory_space=pltpu.VMEM))
        else:
            array, block, index = item if isinstance(item, tuple) else (item, item.shape, None)
            arrays.append(pltpu.with_memory_space_constraint(array, pltpu.HBM))
            specs.append(part(block, index or (0,) * len(block)))
    out_specs = jax.tree.map(
        lambda o: part(o.shape, (0,) * len(o.shape))
        if isinstance(o, jax.ShapeDtypeStruct)
        else pl.BlockSpec(memory_space=pltpu.VMEM),
        outs,
    )
    return pl.pallas_call(
        body,
        out_shape=outs,
        grid=(1,),
        in_specs=specs,
        out_specs=out_specs,
        scratch_shapes=scratch,
        compiler_params=pltpu.CompilerParams(vmem_limit_bytes=16 << 20),
        cost_estimate=pl.CostEstimate(flops=cost[0], bytes_accessed=cost[1], transcendentals=0),
    )(*arrays)


class Near:
    def __init__(self, array):
        self.array = array


def part(shape, index):
    return pl.BlockSpec(tuple(shape), lambda i: tuple(index))


def all_planes(temp, salt, wet, mix, friction, pressure):
    for source in (temp, salt, wet):
        for k in range(levels):
            yield source[k].astype(f32)
    for source in (mix, friction, pressure):
        yield source[...]


def row_pack(planes, up, down):
    at = 0
    for value in planes:
        up[at : at + 2, :] = value[0:2, :]
        down[at : at + 2, :] = value[6:8, :]
        at += 2
    if at < up.shape[0]:
        up[at:, :] = jnp.zeros((up.shape[0] - at, 128), f32)
        down[at:, :] = jnp.zeros((up.shape[0] - at, 128), f32)


def all_rows_body(temp, salt, wet, mix, friction, pressure, up, down):
    row_pack(all_planes(temp, salt, wet, mix, friction, pressure), up, down)


def col_pack(planes, groups, top, bottom, left, right, tall):
    zeros = jnp.zeros((8, 128), f32)
    half = lanes_of((16, 128)) // 2
    for at, value in enumerate(planes):
        tall[at, 0:8, :] = value
        tall[at, 8:16, :] = zeros
        tall[at, 8:10, :] = bottom[2 * at : 2 * at + 2, :]
        tall[at, 14:16, :] = top[2 * at : 2 * at + 2, :]
    start = 0
    for group, count in enumerate(groups):
        go_left = jnp.zeros((16, 128), f32)
        go_right = jnp.zeros((16, 128), f32)
        for k in range(count):
            value = tall[start + k]
            here = half == k
            go_left = jnp.where(here, pltpu.roll(value, 2 * k, 1), go_left)
            go_right = jnp.where(here, pltpu.roll(value, (2 * k + 2) % 128, 1), go_right)
        left[16 * group : 16 * group + 16, :] = go_left
        right[16 * group : 16 * group + 16, :] = go_right
        start += count


def all_cols_body(temp, salt, wet, mix, friction, pressure, top, bottom, left, right, tall):
    planes = all_planes(temp, salt, wet, mix, friction, pressure)
    col_pack(planes, (levels, levels, levels, 3), top, bottom, left, right, tall)


def extended(tall, from_right, from_left, k, dry=False):
    lane = lanes_of((16, 128))
    side = jnp.where(
        lane < 64,
        pltpu.roll(from_right, (128 - 2 * k) % 128, 1),
        pltpu.roll(from_left, 126 - 2 * k, 1),
    )
    if dry:
        side = jnp.where((lane < 2) | (lane >= 126), side, 0.0)
    return jnp.concatenate([tall, side], axis=1)


def beside(value):
    rows, cols = value.shape
    return (
        pltpu.roll(value, 1, 0),
        pltpu.roll(value, rows - 1, 0),
        pltpu.roll(value, 1, 1),
        pltpu.roll(value, cols - 1, 1),
    )


def spread(value, links):
    change = jnp.zeros_like(value)
    for link, near in zip(links, beside(value)):
        change = change + link * (near - value)
    return value + mixing_rate * change


def links_of(wet):
    return tuple(wet * near for near in beside(wet))


def shelf_melt(surface_temp, surface_salt, friction, pressure, wet_top):
    heat_gain = jnp.where(wet_top > 0, friction, 1.0)
    salt_safe = jnp.where(wet_top > 0, surface_salt, 34.0)
    salt_gain = heat_gain / salt_ratio
    curvature = heat_gain * liquidus_slope
    linear = (
        heat_gain * (surface_temp - liquidus_base - liquidus_depth * pressure)
        + latent_ratio * salt_gain
    )
    constant = latent_ratio * salt_gain * salt_safe
    boundary_salt = (
        2.0 * constant / (linear + jnp.sqrt(linear * linear - 4.0 * curvature * constant))
    )
    boundary_temp = liquidus_slope * boundary_salt + liquidus_base + liquidus_depth * pressure
    heat_flux = heat_gain * (surface_temp - boundary_temp) * wet_top
    salt_flux = salt_gain * (salt_safe - boundary_salt) * wet_top
    return heat_flux, salt_flux, boundary_temp * wet_top


def centre_of(value):
    return value[0:8, 0:128]


def surface_body(
    tall, from_right, from_left, slot_row, slot_lane, slot_weight, slot_target, send
):
    def plane(group, k):
        rows = slice(16 * group, 16 * group + 16)
        value = tall[group * levels + k]
        return extended(value, from_right[rows, :], from_left[rows, :], k, group == 2)

    planes = [plane(group, k) for group in range(3) for k in range(few)]
    planes += [plane(3, place) for place in range(3)]
    wets = planes[2 * few : 3 * few]
    mixing, rub, press = planes[9:12]
    first = mixing * (wets[0] * wets[1])
    second = mixing * (wets[1] * wets[2])
    links = [links_of(value) for value in wets]
    stepped = []
    for field in range(2):
        near = [spread(planes[few * field + k], links[k]) for k in range(few)]
        flux = first * (near[1] - near[0])
        under = second * (near[2] - near[1])
        stepped.append((near[0] + flux, near[1] + under - flux))
    heat, brine, base_one = shelf_melt(stepped[0][0], stepped[1][0], rub, press, wets[0])
    tops = (stepped[0][0] - relax_rate * heat, stepped[1][0] - relax_rate * brine)
    later = []
    for field in range(2):
        near0 = spread(tops[field], links[0])
        near1 = spread(stepped[field][1], links[1])
        later.append(centre_of(near0 + first * (near1 - near0)))
    heat_two, unused, base_two = shelf_melt(
        later[0], later[1], centre_of(rub), centre_of(press), centre_of(wets[0])
    )
    melt = 0.5 * (centre_of(heat) / latent_ratio + heat_two / latent_ratio)
    base = 0.5 * (centre_of(base_one) + base_two)

    melts = [jnp.broadcast_to(melt[r : r + 1, :], (8, 128)) for r in range(8)]
    bases = [jnp.broadcast_to(base[r : r + 1, :], (8, 128)) for r in range(8)]

    def owners(i, carry):
        out = send.at[pl.ds(pl.multiple_of(8 * chunk * i, 8), 8 * chunk)]
        for j in range(8):
            at = pl.ds(pl.multiple_of(64 * i + 8 * j, 8), 8)
            lane = slot_lane[at, :]
            row = slot_row[at, :]
            weight = slot_weight[at, :]
            melt_here = jnp.take_along_axis(melts[0], lane, axis=1)
            base_here = jnp.take_along_axis(bases[0], lane, axis=1)
            for r in range(1, 8):
                hit = row == r
                melt_here = jnp.where(
                    hit, jnp.take_along_axis(melts[r], lane, axis=1), melt_here
                )
                base_here = jnp.where(
                    hit, jnp.take_along_axis(bases[r], lane, axis=1), base_here
                )
            out[chunk * j : chunk * j + 8, :] = weight * melt_here
            out[chunk * j + 8 : chunk * j + 16, :] = weight * base_here
            out[chunk * j + 16 : chunk * j + 24, :] = weight
        targets = slot_target[pl.ds(pl.multiple_of(8 * i, 8), 8), :]
        for j in range(8):
            out[chunk * j + 24 : chunk * j + 25, :] = targets[j : j + 1, :]
        return carry

    lax.fori_loop(0, 16, owners, 0)


def slot_body(owner, target, column, weight, slot_row, slot_lane, slot_weight, slot_target):
    count = owner.shape[1]
    row = lax.broadcasted_iota(jnp.int32, (count, count), 0)
    col = lax.broadcasted_iota(jnp.int32, (count, count), 1)
    same = row == col
    owner_lane = owner[...]
    alike = jnp.sum(jnp.where(same, owner_lane, 0), axis=1, keepdims=True) == owner_lane
    rank_lane = jnp.sum(jnp.where(alike & (row < col), 1, 0), axis=0, keepdims=True)
    rank_row = jnp.sum(jnp.where(alike & (col < row), 1, 0), axis=1, keepdims=True)
    target_row = jnp.sum(jnp.where(same, target[...], 0), axis=1, keepdims=True)
    slot = owner_lane * slots + rank_lane
    total = slot_row.shape[0]
    pick = jnp.where(lax.broadcasted_iota(jnp.int32, (total, count), 0) == slot, 1.0, 0.0)
    value = weight[...]
    high = value.astype(bf16)
    rest = value - high.astype(f32)
    middle = rest.astype(bf16)
    low = (rest - middle.astype(f32)).astype(bf16)
    places = column[...]
    table = jnp.concatenate(
        [
            high,
            middle,
            low,
            (places // 128).astype(f32).astype(bf16),
            (places % 128).astype(f32).astype(bf16),
        ],
        axis=1,
    )
    sorted_ = jnp.dot(pick.astype(bf16), table, preferred_element_type=f32)
    slot_weight[...] = sorted_[:, 0:128] + sorted_[:, 128:256] + sorted_[:, 256:384]
    slot_row[...] = sorted_[:, 384:512].astype(jnp.int32)
    slot_lane[...] = sorted_[:, 512:640].astype(jnp.int32)
    lane = lax.broadcasted_iota(jnp.int32, (count, 128), 1)
    spot = jnp.where(rank_row == lane % slots, target_row, 0).astype(f32).astype(bf16)
    holds = jnp.where(lax.broadcasted_iota(jnp.int32, (128, count), 0) == owner_lane, 1.0, 0.0)
    slot_target[...] = jnp.dot(holds.astype(bf16), spot, preferred_element_type=f32)


def ocean_body(
    tall, from_right, from_left, new_temp, new_salt, near, wets, middle_links, later
):
    for end in (0, levels + 1):
        wets[end] = jnp.zeros((16, 256), f32)
        for field in range(2):
            near[field, end] = jnp.zeros((16, 256), f32)
            later[field, end] = jnp.zeros((8, 128), f32)
    mixing, rub, press = (
        extended(tall[3 * levels + p], from_right[48:64, :], from_left[48:64, :], p)
        for p in range(3)
    )

    def group_of(ref, group):
        return ref[16 * group : 16 * group + 16, :]

    def extend(group, k):
        return extended(
            tall[group * levels + k],
            group_of(from_right, group),
            group_of(from_left, group),
            k,
            group == 2,
        )

    unroll = 4

    def spread_level(k):
        water = extend(2, k)
        links = links_of(water)
        wets[k + 1] = water
        for place, link in enumerate(links):
            middle_links[k, place] = centre_of(link)
        for field in range(2):
            near[field, k + 1] = spread(extend(field, k), links)

    def mix_level(k, top):
        water = wets[k + 1]
        under = mixing * (water * wets[k + 2])
        over = mixing * (wets[k] * water)
        once = []
        for field in range(2):
            value = near[field, k + 1]
            value_under = under * (near[field, k + 2] - value)
            value_over = over * (value - near[field, k])
            once.append(value + value_under - value_over)
        if top:
            heat, brine, unused = shelf_melt(once[0], once[1], rub, press, water)
            once = [once[0] - relax_rate * heat, once[1] - relax_rate * brine]
        for field in range(2):
            change = jnp.zeros((8, 128), f32)
            middle = centre_of(once[field])
            for place, side in enumerate(beside(once[field])):
                change = change + middle_links[k, place] * (centre_of(side) - middle)
            later[field, k + 1] = middle + mixing_rate * change

    def finish_level(k, top):
        water = centre_of(wets[k + 1])
        mixing_c = centre_of(mixing)
        under = mixing_c * (water * centre_of(wets[k + 2]))
        over = mixing_c * (centre_of(wets[k]) * water)
        done = []
        for field in range(2):
            value = later[field, k + 1]
            value_under = under * (later[field, k + 2] - value)
            value_over = over * (value - later[field, k])
            done.append(value + value_under - value_over)
        if top:
            heat, brine, unused = shelf_melt(
                done[0], done[1], centre_of(rub), centre_of(press), water
            )
            done = [done[0] - relax_rate * heat, done[1] - relax_rate * brine]
        new_temp[k] = done[0]
        new_salt[k] = done[1]

    def every(step):
        def several(i, carry):
            for j in range(unroll):
                step(unroll * i + j)
            return carry

        lax.fori_loop(0, levels // unroll, several, 0)

    every(spread_level)
    every(lambda k: mix_level(k, False))
    mix_level(0, True)
    every(lambda k: finish_level(k, False))
    finish_level(0, True)


def column_body(enthalpy, surface, transition, offset, factor, pivot_end, side_end):
    count = enthalpy.shape[0]
    side = enthalpy[...].reshape(count, 32, 128)
    change_at = transition[...]
    rates = [jnp.where(k < change_at, cold_rate, temperate_rate) for k in range(count)]
    inner = [0.5 * (rates[k] + rates[k + 1]) for k in range(count - 1)]
    ratios = []
    values = []
    for k in range(count - 1):
        if k == 0:
            pivot = 1.0 + rates[0] + inner[0]
            right = side[0] + rates[0] * surface[...]
        else:
            pivot = 1.0 + inner[k - 1] + inner[k] + inner[k - 1] * ratios[-1]
            right = side[k] + inner[k - 1] * values[-1]
        scale = 1.0 / pivot
        ratios.append(-inner[k] * scale)
        values.append(right * scale)
    pivot_end[...] = 1.0 + inner[-1] + inner[-1] * ratios[-1]
    side_end[...] = side[count - 1] + inner[-1] * values[-1]
    offsets = [jnp.zeros((32, 128), f32)]
    factors = [jnp.ones((32, 128), f32)]
    for k in range(count - 2, -1, -1):
        offsets.append(values[k] - ratios[k] * offsets[-1])
        factors.append(-ratios[k] * factors[-1])
    offset[...] = jnp.stack(offsets[::-1]).reshape(count, 4096)
    factor[...] = jnp.stack(factors[::-1]).reshape(count, 4096)


def collect_body(got, area, offset, factor, pivot_end, side_end, new_enthalpy, melt):
    sums = jnp.zeros((32, 384), f32)
    lane = lax.broadcasted_iota(jnp.int32, (1, 128), 1) // slots
    wanted = lax.broadcasted_iota(jnp.int32, (32, 128), 0).astype(f32)
    for group in range(8):
        parts = ([], [], [])
        target = jnp.zeros((1, 128), f32)
        for s in range(16):
            at = chunk * (16 * group + s)
            for place in range(3):
                parts[place].append(got[at + 8 * place : at + 8 * place + 8, :])
            target = jnp.where(lane == s, got[at + 24 : at + 25, :], target)
        hot = jnp.where(wanted == target, 1.0, 0.0).astype(bf16)
        value = jnp.concatenate([jnp.concatenate(p, axis=0) for p in parts], axis=1)
        high = value.astype(bf16)
        rest = value - high.astype(f32)
        middle = rest.astype(bf16)
        low = (rest - middle.astype(f32)).astype(bf16)
        for piece in (high, middle, low):
            sums = sums + jnp.dot(hot, piece, preferred_element_type=f32)
    size = area[...]
    melt[...] = sums[:, 0:128] / size
    base_sum = sums[:, 128:256] / size
    cover_sum = sums[:, 256:384] / size
    last = (side_end[...] + base_sum) / (pivot_end[...] + cover_sum)
    last = last.reshape(1, 4096)
    new_enthalpy[...] = offset[...] + factor[...] * last


def local(
    ocean_temp,
    ocean_salt,
    wet_mask,
    vertical_mix,
    friction,
    pressure,
    pair_column,
    pair_weight,
    block_owner,
    block_target,
    enthalpy,
    surface_enthalpy,
    transition_layer,
    column_area,
):
    shape = jax.ShapeDtypeStruct
    ocean = (ocean_temp, ocean_salt, wet_mask, vertical_mix, friction, pressure)
    count_x = lax.axis_size("gx")
    count_y = lax.axis_size("gy")
    devices = count_x * count_y

    def chip(*dims, dtype=f32):
        return pltpu.VMEM(dims, dtype)

    def exchange(low, high, axis, count):
        ahead = [(i, i + 1) for i in range(count - 1)]
        back = [(i + 1, i) for i in range(count - 1)]
        return lax.ppermute(low, axis, back), lax.ppermute(high, axis, ahead)

    up, down = call(
        all_rows_body, (chip(halo_rows, 128), chip(halo_rows, 128)), ocean, cost=(10**5, 10**6)
    )
    bottom, top = exchange(up, down, "gy", count_y)
    slot_row, slot_lane, slot_weight, slot_target = call(
        slot_body,
        (
            chip(devices * slots, 128, dtype=jnp.int32),
            chip(devices * slots, 128, dtype=jnp.int32),
            chip(devices * slots, 128),
            chip(devices, 128),
        ),
        (block_owner.reshape(1, -1), block_target.reshape(1, -1), pair_column, pair_weight),
        cost=(2 * 10**9, 3 * 10**6),
    )
    top, slot_target = lax.optimization_barrier((top, slot_target))
    left, right, tall = call(
        all_cols_body,
        (chip(64, 128), chip(64, 128), chip(3 * levels + 3, 16, 128)),
        ocean + (Near(top), Near(bottom)),
        cost=(10**5, 10**6),
    )
    from_right, from_left = exchange(left, right, "gx", count_x)
    send = call(
        surface_body,
        chip(devices * chunk, 128),
        tuple(
            Near(a)
            for a in (tall, from_right, from_left, slot_row, slot_lane, slot_weight, slot_target)
        ),
        cost=(10**6, 3 * 10**6),
    )
    send, from_left, surface_enthalpy = lax.optimization_barrier(
        (send, from_left, surface_enthalpy)
    )
    got = lax.all_to_all(
        send.reshape(devices, chunk, 1, 128),
        ("gx", "gy"),
        split_axis=0,
        concat_axis=0,
        tiled=True,
    ).reshape(devices * chunk, 128)
    new_temp, new_salt = call(
        ocean_body,
        (shape(ocean_temp.shape, f32), shape(ocean_salt.shape, f32)),
        (Near(tall), Near(from_right), Near(from_left)),
        [
            pltpu.VMEM((2, levels + 2, 16, 256), f32),
            pltpu.VMEM((levels + 2, 16, 256), f32),
            pltpu.VMEM((levels, 4, 8, 128), f32),
            pltpu.VMEM((2, levels + 2, 8, 128), f32),
        ],
        cost=(10**8, 2 * 10**6),
    )
    new_temp, surface_enthalpy = lax.optimization_barrier((new_temp, surface_enthalpy))
    offset, factor, pivot_end, side_end = call(
        column_body,
        (chip(*enthalpy.shape), chip(*enthalpy.shape), chip(32, 128), chip(32, 128)),
        (enthalpy, surface_enthalpy.reshape(32, 128), transition_layer.reshape(32, 128)),
        cost=(10**8, 2 * 10**6),
    )
    new_enthalpy, melt = call(
        collect_body,
        (shape(enthalpy.shape, f32), shape((32, 128), f32)),
        (
            Near(got),
            column_area.reshape(32, 128),
            Near(offset),
            Near(factor),
            Near(pivot_end),
            Near(side_end),
        ),
        cost=(10**9, 4 * 10**6),
    )
    return new_temp, new_salt, new_enthalpy, melt.reshape(-1)


def solution(mesh):
    return jax.shard_map(
        local,
        mesh=mesh,
        in_specs=(
            P(None, "gy", "gx"),
            P(None, "gy", "gx"),
            P(None, "gy", "gx"),
            P("gy", "gx"),
            P("gy", "gx"),
            P("gy", "gx"),
            P(("gx", "gy"), None),
            P(("gx", "gy"), None),
            P(("gx", "gy"), None),
            P(("gx", "gy")),
            P(None, ("gx", "gy")),
            P(("gx", "gy")),
            P(("gx", "gy")),
            P(("gx", "gy")),
        ),
        out_specs=(
            P(None, "gy", "gx"),
            P(None, "gy", "gx"),
            P(None, ("gx", "gy")),
            P(("gx", "gy")),
        ),
        check_vma=False,
    )
```

time: 76.4 us -> 67.9 us (0.89)
  Pallas kernels: 39.3 us -> 23.5 us
  waiting for transfers between devices: 8.68 us -> 18.9 us
  local copies, waits for them, and re-layouts: 4.03 us -> 0 us
  starting transfers between devices: 23.3 us -> 24.3 us
    pallas_call x7, Pallas kernels: 39.3 us -> 23.5 us  [call(): pl.pallas_call(body, out_shape=outs, grid=(1,), in_specs=specs, out_specs...]
    all_to_all x1, waiting for transfers between devices: 4.9 us -> 15.5 us  [local(): lax.all_to_all(send.reshape(devices, chunk, 1, 128), ('gx', 'gy'), split_...]
    unnamed x11 -> x0, local copies, waits for them, and re-layouts: 4.03 us -> none
    all_to_all x1, starting transfers between devices: 11.6 us -> 12.6 us  [local(): lax.all_to_all(send.reshape(devices, chunk, 1, 128), ('gx', 'gy'), split_...]
  transfers between devices with their start and end apart: 5 -> 5, of which waited for: 2 -> 3; matrix products, arithmetic and copies ran while one was open for 2% -> 0% of each run, Pallas kernels for 32% -> 19%
where the time goes in v2:
time: 67.9 us; the launch traced here: 67.5 us
  starting transfers between devices  24.3 us (36%)
  Pallas kernels  23.5 us (35%)
  waiting for transfers between devices  18.9 us (28%)
  between operations  0.71 us (1%)
    pallas_call x7, Pallas kernels, call(): pl.pallas_call(body, out_shape=outs, grid=(1,), in_specs=specs, out_specs...  23.5 us
    all_to_all x1, waiting for transfers between devices, local(): lax.all_to_all(send.reshape(devices, chunk, 1, 128), ('gx', 'gy'), split_...  15.5 us
    all_to_all x1, starting transfers between devices, local(): lax.all_to_all(send.reshape(devices, chunk, 1, 128), ('gx', 'gy'), split_...  12.6 us
    ppermute x4, starting transfers between devices, exchange(): return (lax.ppermute(low, axis, back), lax.ppermute(high, axis, ahead))  11.7 us
    ppermute x4, waiting for transfers between devices, exchange(): return (lax.ppermute(low, axis, back), lax.ppermute(high, axis, ahead))  3.45 us
  transfers between devices with their start and end apart: 5, of which 3 were waited for; matrix products, arithmetic and copies ran while one was open for 0% of the time, Pallas kernels for 19%

profile of v2, /device:TPU:1, one launch (start us, length us, event | category | flops | bytes accessed | tf_op | source)
XLA Modules:
  0.0 67.5 jit_solution(6499717824593768851)
XLA Ops:
  0.6 1.2 %shard_map.165 = (f32[392,128]{1,0:T(8,128)S(1)}, f32[392,128]{1,0:T(8,128)S(1)}) custom-call(f32[64,8,128]{2,1,0:T(8,128)} %temp.3, f32[64,8,128]{2,1,0:T(8,128)} %salt.3, s32[64,8,128]{2,1,0:T(8,128)} %wet.3, f32[8,128]{1,0:T(8,128)} %mix.3, f32[8,128]{1,0:T(8,128)} %friction.3, f32[8,128]{1,0:T(8,128)} %pressure.3), custom_call_target="tpu_custom_call" | custom-call | flops 100000 | bytes 1000000 | tf_op jit(solution)/shard_map/pallas_call | solution.py:47
  1.9 4.5 %collective-permute-start = (f32[392,128]{1,0:T(8,128)S(1)}, f32[392,128]{1,0:T(8,128)S(1)}, u32[]{:S(2)}, u32[]{:S(2)}) collective-permute-start(f32[392,128]{1,0:T(8,128)S(1)} %get-tuple-element.28), channel_id=1, source_target_pairs={{0,1},{1,2},{2,3},{3,4},{4,5},{5,6},{6,7},{8,9},{9,10},{10,11},{11... | collective-permute-start | bytes 602120 | tf_op jit(solution)/shard_map/ppermute | solution.py:454
  6.4 1.9 %collective-permute-start.1 = (f32[392,128]{1,0:T(8,128)S(1)}, f32[392,128]{1,0:T(8,128)S(1)}, u32[]{:S(2)}, u32[]{:S(2)}) collective-permute-start(f32[392,128]{1,0:T(8,128)S(1)} %get-tuple-element.31), channel_id=1, source_target_pairs={{1,0},{2,1},{3,2},{4,3},{5,4},{6,5},{7,6},{9,8},{10,9},{11,10},{12... | collective-permute-start | bytes 602120 | tf_op jit(solution)/shard_map/ppermute | solution.py:454
  8.3 2.6 %shard_map.166 = (s32[1024,128]{1,0:T(8,128)S(1)}, s32[1024,128]{1,0:T(8,128)S(1)}, f32[1024,128]{1,0:T(8,128)S(1)}, f32[128,128]{1,0:T(8,128)S(1)}) custom-call(s32[1,512]{1,0:T(1,128)} %bitcast.12, s32[1,512]{1,0:T(1,128)} %bitcast.13, s32[512,128]{1,0:T(8,128)} %column.1, f32[512,128]{1,0:T(8,128)} %weight.1), custom_call_target="tpu_custom_call" | custom-call | flops 2000000000 | bytes 3000000 | tf_op jit(solution)/shard_map/pallas_call | solution.py:47
  10.9 0.0 collective-permute-done.top
  11.0 2.5 %collective-permute-done.1.bottom = f32[392,128]{1,0:T(8,128)S(1)} collective-permute-done((f32[392,128]{1,0:T(8,128)S(1)}, f32[392,128]{1,0:T(8,128)S(1)}, u32[]{:S(2)}, u32[]{:S(2)}) %collective-permute-start.1) | collective-permute-done | bytes 200736 | tf_op jit(solution)/shard_map/ppermute | solution.py:454
  13.4 2.1 %shard_map.167 = (f32[64,128]{1,0:T(8,128)S(1)}, f32[64,128]{1,0:T(8,128)S(1)}, f32[195,16,128]{2,1,0:T(8,128)S(1)}) custom-call(f32[64,8,128]{2,1,0:T(8,128)} %temp.3, f32[64,8,128]{2,1,0:T(8,128)} %salt.3, s32[64,8,128]{2,1,0:T(8,128)} %wet.3, f32[8,128]{1,0:T(8,128)} %mix.3, f32[8,128]{1,0:T(8,128)} %friction.3, f32[8,128]{1,0:T(8,128)} %pressure.3, ...), custom_call_target="tpu_custom_call" | custom-call | flops 100000 | bytes 1000000 | tf_op jit(solution)/shard_map/pallas_call | solution.py:47
  15.6 1.3 %collective-permute-start.2 = (f32[64,128]{1,0:T(8,128)S(1)}, f32[64,128]{1,0:T(8,128)S(1)}, u32[]{:S(2)}, u32[]{:S(2)}) collective-permute-start(f32[64,128]{1,0:T(8,128)S(1)} %get-tuple-element.33), channel_id=1, source_target_pairs={{8,0},{16,8},{24,16},{32,24},{40,32},{48,40},{56,48},{64,56},{72,6... | collective-permute-start | bytes 98312 | tf_op jit(solution)/shard_map/ppermute | solution.py:454
  16.9 4.0 %collective-permute-start.3 = (f32[64,128]{1,0:T(8,128)S(1)}, f32[64,128]{1,0:T(8,128)S(1)}, u32[]{:S(2)}, u32[]{:S(2)}) collective-permute-start(f32[64,128]{1,0:T(8,128)S(1)} %get-tuple-element.34), channel_id=1, source_target_pairs={{0,8},{8,16},{16,24},{24,32},{32,40},{40,48},{48,56},{56,64},{64,7... | collective-permute-start | bytes 98312 | tf_op jit(solution)/shard_map/ppermute | solution.py:454
  20.8 0.0 collective-permute-done.2.from_right
  20.9 1.0 %collective-permute-done.3.from_left = f32[64,128]{1,0:T(8,128)S(1)} collective-permute-done((f32[64,128]{1,0:T(8,128)S(1)}, f32[64,128]{1,0:T(8,128)S(1)}, u32[]{:S(2)}, u32[]{:S(2)}) %collective-permute-start.3) | collective-permute-done | bytes 32800 | tf_op jit(solution)/shard_map/ppermute | solution.py:454
  21.9 5.2 %shard_map.168 = f32[3200,128]{1,0:T(8,128)} custom-call(f32[195,16,128]{2,1,0:T(8,128)S(1)} %get-tuple-element.32.tall, f32[64,128]{1,0:T(8,128)S(1)} %collective-permute-done.2.from_right, f32[64,128]{1,0:T(8,128)S(1)} %collective-permute-done.3.from_left, s32[1024,128]{1,0:T(8,128)S(1)} %get-tuple-element.35.slot_row, ...), custom_call_target="tpu_custom_call" | custom-call | flops 1000000 | bytes 3000000 | tf_op jit(solution)/shard_map/pallas_call | solution.py:47
  27.1 12.6 %all-to-all-start = ((f32[128,25,1,128]{3,2,1,0:T(1,128)}), f32[128,25,1,128]{3,2,1,0:T(1,128)S(1)}, u32[]{:S(2)}, u32[]{:S(2)}) async-start(f32[128,25,1,128]{3,2,1,0:T(1,128)} %bitcast.2), calls=%async_computation | async-start | bytes 3276800 | tf_op jit(solution)/shard_map/all_to_all | solution.py:491
  39.7 8.1 %shard_map.169 = (f32[64,8,128]{2,1,0:T(8,128)}, f32[64,8,128]{2,1,0:T(8,128)}) custom-call(f32[195,16,128]{2,1,0:T(8,128)S(1)} %get-tuple-element.32.tall, f32[64,128]{1,0:T(8,128)S(1)} %collective-permute-done.2.from_right, f32[64,128]{1,0:T(8,128)S(1)} %collective-permute-done.3.from_left), custom_call_target="tpu_custom_call" | custom-call | flops 100000000 | bytes 2000000 | tf_op jit(solution)/shard_map/pallas_call | solution.py:47
  47.8 1.9 %shard_map.170 = (f32[40,4096]{1,0:T(8,128)S(1)}, f32[40,4096]{1,0:T(8,128)S(1)}, f32[32,128]{1,0:T(8,128)S(1)}, f32[32,128]{1,0:T(8,128)S(1)}) custom-call(f32[40,4096]{1,0:T(8,128)} %enthalpy.1, f32[32,128]{1,0:T(8,128)} %bitcast.9, s32[32,128]{1,0:T(8,128)} %bitcast.10), custom_call_target="tpu_custom_call" | custom-call | flops 100000000 | bytes 2000000 | tf_op jit(solution)/shard_map/pallas_call | solution.py:47
  49.8 15.5 %all-to-all-done = f32[128,25,1,128]{3,2,1,0:T(1,128)S(1)} async-done(((f32[128,25,1,128]{3,2,1,0:T(1,128)}), f32[128,25,1,128]{3,2,1,0:T(1,128)S(1)}, u32[]{:S(2)}, u32[]{:S(2)}) %all-to-all-start) | async-done | bytes 1638432 | tf_op jit(solution)/shard_map/all_to_all | solution.py:491
  65.3 2.2 %shard_map.171 = (f32[40,4096]{1,0:T(8,128)}, f32[32,128]{1,0:T(8,128)}) custom-call(f32[3200,128]{1,0:T(8,128)S(1)} %bitcast.8, f32[32,128]{1,0:T(8,128)} %bitcast.11, f32[40,4096]{1,0:T(8,128)S(1)} %get-tuple-element.46.offset, f32[40,4096]{1,0:T(8,128)S(1)} %get-tuple-element.47.factor, f32[32,128]{1,0:T(8,128)S(1)} %get-tuple-element.48.pivot_end, ...), custom_call_target="tpu_custom_call" | custom-call | flops 1000000000 | bytes 4000000 | tf_op jit(solution)/shard_map/pallas_call | solution.py:47
Async XLA Ops:
  1.9 9.1 %collective-permute-start = (f32[392,128]{1,0:T(8,128)S(1)}, f32[392,128]{1,0:T(8,128)S(1)}, u32[]{:S(2)}, u32[]{:S(2)}) collective-permute-start(f32[392,128]{1,0:T(8,128)S(1)} %get-tuple-element.28), channel_id=1, source_target_pairs={{0,1},{1,2},{2,3},{3,4},{4,5},{5,6},{6,7},{8,9},{9,10},{10,11},{11... | collective-permute-start | bytes 602120 | tf_op jit(solution)/shard_map/ppermute | solution.py:454
  6.4 7.0 %collective-permute-start.1 = (f32[392,128]{1,0:T(8,128)S(1)}, f32[392,128]{1,0:T(8,128)S(1)}, u32[]{:S(2)}, u32[]{:S(2)}) collective-permute-start(f32[392,128]{1,0:T(8,128)S(1)} %get-tuple-element.31), channel_id=1, source_target_pairs={{1,0},{2,1},{3,2},{4,3},{5,4},{6,5},{7,6},{9,8},{10,9},{11,10},{12... | collective-permute-start | bytes 602120 | tf_op jit(solution)/shard_map/ppermute | solution.py:454
  15.6 5.3 %collective-permute-start.2 = (f32[64,128]{1,0:T(8,128)S(1)}, f32[64,128]{1,0:T(8,128)S(1)}, u32[]{:S(2)}, u32[]{:S(2)}) collective-permute-start(f32[64,128]{1,0:T(8,128)S(1)} %get-tuple-element.33), channel_id=1, source_target_pairs={{8,0},{16,8},{24,16},{32,24},{40,32},{48,40},{56,48},{64,56},{72,6... | collective-permute-start | bytes 98312 | tf_op jit(solution)/shard_map/ppermute | solution.py:454
  16.9 5.0 %collective-permute-start.3 = (f32[64,128]{1,0:T(8,128)S(1)}, f32[64,128]{1,0:T(8,128)S(1)}, u32[]{:S(2)}, u32[]{:S(2)}) collective-permute-start(f32[64,128]{1,0:T(8,128)S(1)} %get-tuple-element.34), channel_id=1, source_target_pairs={{0,8},{8,16},{16,24},{24,32},{32,40},{40,48},{48,56},{56,64},{64,7... | collective-permute-start | bytes 98312 | tf_op jit(solution)/shard_map/ppermute | solution.py:454
  27.1 38.2 %all-to-all-start = ((f32[128,25,1,128]{3,2,1,0:T(1,128)}), f32[128,25,1,128]{3,2,1,0:T(1,128)S(1)}, u32[]{:S(2)}, u32[]{:S(2)}) async-start(f32[128,25,1,128]{3,2,1,0:T(1,128)} %bitcast.2), calls=%async_computation | async-start | bytes 3276800 | tf_op jit(solution)/shard_map/all_to_all | solution.py:491

commit v3 on v2

--- a/solution.py
+++ b/solution.py
@@ -22,13 +22,14 @@
 chunk = 3 * slots + 1
 halo_rows = 392
 few = 3
+batch = 16
 
 
 def lanes_of(shape):
     return lax.broadcasted_iota(jnp.int32, shape, len(shape) - 1)
 
 
-def call(body, outs, ins, scratch=(), cost=(0, 0)):
+def call(body, outs, ins, scratch=(), cost=(0, 0), own_copies=False):
     arrays, specs = [], []
     for item in ins:
         if isinstance(item, Near):
@@ -38,12 +39,15 @@
             array, block, index = item if isinstance(item, tuple) else (item, item.shape, None)
             arrays.append(pltpu.with_memory_space_constraint(array, pltpu.HBM))
             specs.append(part(block, index or (0,) * len(block)))
-    out_specs = jax.tree.map(
-        lambda o: part(o.shape, (0,) * len(o.shape))
-        if isinstance(o, jax.ShapeDtypeStruct)
-        else pl.BlockSpec(memory_space=pltpu.VMEM),
-        outs,
-    )
+    if own_copies:
+        out_specs = pl.BlockSpec(memory_space=pltpu.HBM)
+    else:
+        out_specs = jax.tree.map(
+            lambda o: part(o.shape, (0,) * len(o.shape))
+            if isinstance(o, jax.ShapeDtypeStruct)
+            else pl.BlockSpec(memory_space=pltpu.VMEM),
+            outs,
+        )
     return pl.pallas_call(
         body,
         out_shape=outs,
@@ -73,46 +77,60 @@
         yield source[...]
 
 
-def row_pack(planes, up, down):
+def even_on(axis):
+    return lax.axis_index(axis) % 2 == 0
+
+
+def row_pack(planes, first, second):
+    even = even_on("gy")
     at = 0
     for value in planes:
-        up[at : at + 2, :] = value[0:2, :]
-        down[at : at + 2, :] = value[6:8, :]
+        high, low = value[6:8, :], value[0:2, :]
+        first[at : at + 2, :] = jnp.where(even, high, low)
+        second[at : at + 2, :] = jnp.where(even, low, high)
         at += 2
-    if at < up.shape[0]:
-        up[at:, :] = jnp.zeros((up.shape[0] - at, 128), f32)
-        down[at:, :] = jnp.zeros((up.shape[0] - at, 128), f32)
-
-
-def all_rows_body(temp, salt, wet, mix, friction, pressure, up, down):
-    row_pack(all_planes(temp, salt, wet, mix, friction, pressure), up, down)
-
-
-def col_pack(planes, groups, top, bottom, left, right, tall):
+    first[at:, :] = jnp.zeros((first.shape[0] - at, 128), f32)
+    second[at:, :] = jnp.zeros((first.shape[0] - at, 128), f32)
+
+
+def all_rows_body(temp, salt, wet, mix, friction, pressure, first, second):
+    row_pack(all_planes(temp, salt, wet, mix, friction, pressure), first, second)
+
+
+def col_pack(planes, groups, rows_first, rows_second, first, second, tall):
     zeros = jnp.zeros((8, 128), f32)
     half = lanes_of((16, 128)) // 2
+    at_first = jnp.where(even_on("gy"), 8, 14)
+    at_second = 22 - at_first
     for at, value in enumerate(planes):
         tall[at, 0:8, :] = value
         tall[at, 8:16, :] = zeros
-        tall[at, 8:10, :] = bottom[2 * at : 2 * at + 2, :]
-        tall[at, 14:16, :] = top[2 * at : 2 * at + 2, :]
+        tall[at, pl.ds(at_first, 2), :] = rows_first[2 * at : 2 * at + 2, :]
+        tall[at, pl.ds(at_second, 2), :] = rows_second[2 * at : 2 * at + 2, :]
+    even = even_on("gx")
     start = 0
     for group, count in enumerate(groups):
-        go_left = jnp.zeros((16, 128), f32)
-        go_right = jnp.zeros((16, 128), f32)
+        low = jnp.zeros((16, 128), f32)
+        high = jnp.zeros((16, 128), f32)
         for k in range(count):
             value = tall[start + k]
             here = half == k
-            go_left = jnp.where(here, pltpu.roll(value, 2 * k, 1), go_left)
-            go_right = jnp.where(here, pltpu.roll(value, (2 * k + 2) % 128, 1), go_right)
-        left[16 * group : 16 * group + 16, :] = go_left
-        right[16 * group : 16 * group + 16, :] = go_right
+            low = jnp.where(here, pltpu.roll(value, 2 * k, 1), low)
+            high = jnp.where(here, pltpu.roll(value, (2 * k + 2) % 128, 1), high)
+        first[16 * group : 16 * group + 16, :] = jnp.where(even, high, low)
+        second[16 * group : 16 * group + 16, :] = jnp.where(even, low, high)
         start += count
 
 
-def all_cols_body(temp, salt, wet, mix, friction, pressure, top, bottom, left, right, tall):
+def sides_received(first, second):
+    even = even_on("gx")
+    return jnp.where(even, first, second), jnp.where(even, second, first)
+
+
+def all_cols_body(temp, salt, wet, mix, friction, pressure, rows_first, rows_second, first, second, tall):
     planes = all_planes(temp, salt, wet, mix, friction, pressure)
-    col_pack(planes, (levels, levels, levels, 3), top, bottom, left, right, tall)
+    groups = (levels, levels, levels, 3)
+    col_pack(planes, groups, rows_first, rows_second, first, second, tall)
 
 
 def extended(tall, from_right, from_left, k, dry=False):
@@ -172,12 +190,14 @@
 
 
 def surface_body(
-    tall, from_right, from_left, slot_row, slot_lane, slot_weight, slot_target, send
+    tall, cols_first, cols_second, slot_row, slot_lane, slot_weight, slot_target, send, held, sems
 ):
+    from_right, from_left = sides_received(cols_first[...], cols_second[...])
+
     def plane(group, k):
         rows = slice(16 * group, 16 * group + 16)
         value = tall[group * levels + k]
-        return extended(value, from_right[rows, :], from_left[rows, :], k, group == 2)
+        return extended(value, from_right[rows], from_left[rows], k, group == 2)
 
     planes = [plane(group, k) for group in range(3) for k in range(few)]
     planes += [plane(3, place) for place in range(3)]
@@ -208,10 +228,15 @@
     melts = [jnp.broadcast_to(melt[r : r + 1, :], (8, 128)) for r in range(8)]
     bases = [jnp.broadcast_to(base[r : r + 1, :], (8, 128)) for r in range(8)]
 
+    def leave(i):
+        rows = pl.ds(pl.multiple_of(chunk * batch * i, 8), chunk * batch)
+        return pltpu.make_async_copy(held.at[rows], send.at[rows], sems.at[i])
+
     def owners(i, carry):
-        out = send.at[pl.ds(pl.multiple_of(8 * chunk * i, 8), 8 * chunk)]
-        for j in range(8):
-            at = pl.ds(pl.multiple_of(64 * i + 8 * j, 8), 8)
+        out = held.at[pl.ds(pl.multiple_of(chunk * batch * i, 8), chunk * batch)]
+        targets = slot_target[pl.ds(pl.multiple_of(batch * i, 8), batch), :]
+        for j in range(batch):
+            at = pl.ds(pl.multiple_of(8 * batch * i + 8 * j, 8), 8)
             lane = slot_lane[at, :]
             row = slot_row[at, :]
             weight = slot_weight[at, :]
@@ -228,12 +253,14 @@
             out[chunk * j : chunk * j + 8, :] = weight * melt_here
             out[chunk * j + 8 : chunk * j + 16, :] = weight * base_here
             out[chunk * j + 16 : chunk * j + 24, :] = weight
-        targets = slot_target[pl.ds(pl.multiple_of(8 * i, 8), 8), :]
-        for j in range(8):
             out[chunk * j + 24 : chunk * j + 25, :] = targets[j : j + 1, :]
+        leave(i).start()
         return carry
 
-    lax.fori_loop(0, 16, owners, 0)
+    count = slot_target.shape[0] // batch
+    lax.fori_loop(0, count, owners, 0)
+    for i in range(count):
+        leave(i).wait()
 
 
 def slot_body(owner, target, column, weight, slot_row, slot_lane, slot_weight, slot_target):
@@ -276,8 +303,19 @@
 
 
 def ocean_body(
-    tall, from_right, from_left, new_temp, new_salt, near, wets, middle_links, later
+    tall,
+    cols_first,
+    cols_second,
+    new_temp,
+    new_salt,
+    near,
+    wets,
+    middle_links,
+    later,
+    from_right,
+    from_left,
 ):
+    from_right[...], from_left[...] = sides_received(cols_first[...], cols_second[...])
     for end in (0, levels + 1):
         wets[end] = jnp.zeros((16, 256), f32)
         for field in range(2):
@@ -448,15 +486,15 @@
     def chip(*dims, dtype=f32):
         return pltpu.VMEM(dims, dtype)
 
-    def exchange(low, high, axis, count):
-        ahead = [(i, i + 1) for i in range(count - 1)]
-        back = [(i + 1, i) for i in range(count - 1)]
-        return lax.ppermute(low, axis, back), lax.ppermute(high, axis, ahead)
-
-    up, down = call(
+    def exchange(first, second, axis, count):
+        pairs = [(i, i ^ 1) for i in range(count)]
+        later = [(i + 1, (i ^ 1) + 1) for i in range(count - 2)]
+        return lax.ppermute(first, axis, pairs), lax.ppermute(second, axis, later)
+
+    rows_first, rows_second = call(
         all_rows_body, (chip(halo_rows, 128), chip(halo_rows, 128)), ocean, cost=(10**5, 10**6)
     )
-    bottom, top = exchange(up, down, "gy", count_y)
+    rows_first, rows_second = exchange(rows_first, rows_second, "gy", count_y)
     slot_row, slot_lane, slot_weight, slot_target = call(
         slot_body,
         (
@@ -468,25 +506,35 @@
         (block_owner.reshape(1, -1), block_target.reshape(1, -1), pair_column, pair_weight),
         cost=(2 * 10**9, 3 * 10**6),
     )
-    top, slot_target = lax.optimization_barrier((top, slot_target))
-    left, right, tall = call(
+    rows_first, slot_target = lax.optimization_barrier((rows_first, slot_target))
+    cols_first, cols_second, tall = call(
         all_cols_body,
         (chip(64, 128), chip(64, 128), chip(3 * levels + 3, 16, 128)),
-        ocean + (Near(top), Near(bottom)),
+        ocean + (Near(rows_first), Near(rows_second)),
         cost=(10**5, 10**6),
     )
-    from_right, from_left = exchange(left, right, "gx", count_x)
+    cols_first, cols_second = exchange(cols_first, cols_second, "gx", count_x)
     send = call(
         surface_body,
-        chip(devices * chunk, 128),
+        shape((devices * chunk, 128), f32),
         tuple(
             Near(a)
-            for a in (tall, from_right, from_left, slot_row, slot_lane, slot_weight, slot_target)
+            for a in (
+                tall,
+                cols_first,
+                cols_second,
+                slot_row,
+                slot_lane,
+                slot_weight,
+                slot_target,
+            )
         ),
+        [pltpu.VMEM((devices * chunk, 128), f32), pltpu.SemaphoreType.DMA((devices // batch,))],
         cost=(10**6, 3 * 10**6),
-    )
-    send, from_left, surface_enthalpy = lax.optimization_barrier(
-        (send, from_left, surface_enthalpy)
+        own_copies=True,
+    )
+    send, cols_first, surface_enthalpy = lax.optimization_barrier(
+        (send, cols_first, surface_enthalpy)
     )
     got = lax.all_to_all(
         send.reshape(devices, chunk, 1, 128),
@@ -498,12 +546,14 @@
     new_temp, new_salt = call(
         ocean_body,
         (shape(ocean_temp.shape, f32), shape(ocean_salt.shape, f32)),
-        (Near(tall), Near(from_right), Near(from_left)),
+        (Near(tall), Near(cols_first), Near(cols_second)),
         [
             pltpu.VMEM((2, levels + 2, 16, 256), f32),
             pltpu.VMEM((levels + 2, 16, 256), f32),
             pltpu.VMEM((levels, 4, 8, 128), f32),
             pltpu.VMEM((2, levels + 2, 8, 128), f32),
+            pltpu.VMEM((64, 128), f32),
+            pltpu.VMEM((64, 128), f32),
         ],
         cost=(10**8, 2 * 10**6),
     )

time: 67.9 us -> 63.4 us (0.934)
  starting transfers between devices: 24.3 us -> 22.4 us
  waiting for transfers between devices: 18.9 us -> 17.4 us
  Pallas kernels: 23.5 us -> 22.6 us
    ppermute x4, starting transfers between devices: 11.7 us -> 6.73 us  [exchange(): return (lax.ppermute(first, axis, pairs), lax.ppermute(second, axis, later))]
    all_to_all x1, starting transfers between devices: 12.6 us -> 15.7 us  [local(): lax.all_to_all(send.reshape(devices, chunk, 1, 128), ('gx', 'gy'), split_...]
    ppermute x4, waiting for transfers between devices: 3.45 us -> 1.94 us  [exchange(): return (lax.ppermute(first, axis, pairs), lax.ppermute(second, axis, later))]
    pallas_call x7, Pallas kernels: 23.5 us -> 22.6 us  [call(): pl.pallas_call(body, out_shape=outs, grid=(1,), in_specs=specs, out_specs...]
  transfers between devices with their start and end apart: 5 -> 5, of which waited for: 3 -> 3; matrix products, arithmetic and copies ran while one was open for 0% -> 0% of each run, Pallas kernels for 19% -> 20%
where the time goes in v3:
time: 63.4 us; the launch traced here: 63.1 us
  Pallas kernels  22.6 us (36%)
  starting transfers between devices  22.4 us (35%)
  waiting for transfers between devices  17.4 us (27%)
  between operations  0.7 us (1%)
    pallas_call x7, Pallas kernels, call(): pl.pallas_call(body, out_shape=outs, grid=(1,), in_specs=specs, out_specs...  22.6 us
    all_to_all x1, starting transfers between devices, local(): lax.all_to_all(send.reshape(devices, chunk, 1, 128), ('gx', 'gy'), split_...  15.7 us
    all_to_all x1, waiting for transfers between devices, local(): lax.all_to_all(send.reshape(devices, chunk, 1, 128), ('gx', 'gy'), split_...  15.5 us
    ppermute x4, starting transfers between devices, exchange(): return (lax.ppermute(first, axis, pairs), lax.ppermute(second, axis, later))  6.73 us
    ppermute x4, waiting for transfers between devices, exchange(): return (lax.ppermute(first, axis, pairs), lax.ppermute(second, axis, later))  1.94 us
  transfers between devices with their start and end apart: 5, of which 3 were waited for; matrix products, arithmetic and copies ran while one was open for 0% of the time, Pallas kernels for 20%

profile of v3, /device:TPU:1, one launch (start us, length us, event | category | flops | bytes accessed | tf_op | source)
XLA Modules:
  0.0 63.1 jit_solution(12702355132752593290)
XLA Ops:
  0.6 1.3 %shard_map.165 = (f32[392,128]{1,0:T(8,128)S(1)}, f32[392,128]{1,0:T(8,128)S(1)}) custom-call(f32[64,8,128]{2,1,0:T(8,128)} %temp.3, f32[64,8,128]{2,1,0:T(8,128)} %salt.3, s32[64,8,128]{2,1,0:T(8,128)} %wet.3, f32[8,128]{1,0:T(8,128)} %mix.3, f32[8,128]{1,0:T(8,128)} %friction.3, f32[8,128]{1,0:T(8,128)} %pressure.3), custom_call_target="tpu_custom_call" | custom-call | flops 100000 | bytes 1000000 | tf_op jit(solution)/shard_map/pallas_call | solution.py:51
  1.9 1.5 %collective-permute-start = (f32[392,128]{1,0:T(8,128)S(1)}, f32[392,128]{1,0:T(8,128)S(1)}, u32[]{:S(2)}, u32[]{:S(2)}) collective-permute-start(f32[392,128]{1,0:T(8,128)S(1)} %get-tuple-element.28), channel_id=1, source_target_pairs={{0,1},{1,0},{2,3},{3,2},{4,5},{5,4},{6,7},{7,6},{8,9},{9,8},{10,11... | collective-permute-start | bytes 602120 | tf_op jit(solution)/shard_map/ppermute | solution.py:492
  3.4 3.1 %collective-permute-start.1 = (f32[392,128]{1,0:T(8,128)S(1)}, f32[392,128]{1,0:T(8,128)S(1)}, u32[]{:S(2)}, u32[]{:S(2)}) collective-permute-start(f32[392,128]{1,0:T(8,128)S(1)} %get-tuple-element.31), channel_id=1, source_target_pairs={{1,2},{2,1},{3,4},{4,3},{5,6},{6,5},{9,10},{10,9},{11,12},{12,11},... | collective-permute-start | bytes 602120 | tf_op jit(solution)/shard_map/ppermute | solution.py:492
  6.5 2.6 %shard_map.166 = (s32[1024,128]{1,0:T(8,128)S(1)}, s32[1024,128]{1,0:T(8,128)S(1)}, f32[1024,128]{1,0:T(8,128)S(1)}, f32[128,128]{1,0:T(8,128)S(1)}) custom-call(s32[1,512]{1,0:T(1,128)} %bitcast.12, s32[1,512]{1,0:T(1,128)} %bitcast.13, s32[512,128]{1,0:T(8,128)} %column.1, f32[512,128]{1,0:T(8,128)} %weight.1), custom_call_target="tpu_custom_call" | custom-call | flops 2000000000 | bytes 3000000 | tf_op jit(solution)/shard_map/pallas_call | solution.py:51
  9.1 0.0 collective-permute-done.rows_first
  9.1 1.2 %collective-permute-done.1.rows_second = f32[392,128]{1,0:T(8,128)S(1)} collective-permute-done((f32[392,128]{1,0:T(8,128)S(1)}, f32[392,128]{1,0:T(8,128)S(1)}, u32[]{:S(2)}, u32[]{:S(2)}) %collective-permute-start.1) | collective-permute-done | bytes 200736 | tf_op jit(solution)/shard_map/ppermute | solution.py:492
  10.4 2.2 %shard_map.167 = (f32[64,128]{1,0:T(8,128)S(1)}, f32[64,128]{1,0:T(8,128)S(1)}, f32[195,16,128]{2,1,0:T(8,128)S(1)}) custom-call(f32[64,8,128]{2,1,0:T(8,128)} %temp.3, f32[64,8,128]{2,1,0:T(8,128)} %salt.3, s32[64,8,128]{2,1,0:T(8,128)} %wet.3, f32[8,128]{1,0:T(8,128)} %mix.3, f32[8,128]{1,0:T(8,128)} %friction.3, f32[8,128]{1,0:T(8,128)} %pressure.3, ...), custom_call_target="tpu_custom_call" | custom-call | flops 100000 | bytes 1000000 | tf_op jit(solution)/shard_map/pallas_call | solution.py:51
  12.6 1.5 %collective-permute-start.2 = (f32[64,128]{1,0:T(8,128)S(1)}, f32[64,128]{1,0:T(8,128)S(1)}, u32[]{:S(2)}, u32[]{:S(2)}) collective-permute-start(f32[64,128]{1,0:T(8,128)S(1)} %get-tuple-element.33), channel_id=1, source_target_pairs={{0,8},{8,0},{16,24},{24,16},{32,40},{40,32},{48,56},{56,48},{64,72... | collective-permute-start | bytes 98312 | tf_op jit(solution)/shard_map/ppermute | solution.py:492
  14.1 0.7 %collective-permute-start.3 = (f32[64,128]{1,0:T(8,128)S(1)}, f32[64,128]{1,0:T(8,128)S(1)}, u32[]{:S(2)}, u32[]{:S(2)}) collective-permute-start(f32[64,128]{1,0:T(8,128)S(1)} %get-tuple-element.34), channel_id=1, source_target_pairs={{8,16},{16,8},{24,32},{32,24},{40,48},{48,40},{56,64},{64,56},{72,... | collective-permute-start | bytes 98312 | tf_op jit(solution)/shard_map/ppermute | solution.py:492
  14.7 0.7 %collective-permute-done.2.cols_first = f32[64,128]{1,0:T(8,128)S(1)} collective-permute-done((f32[64,128]{1,0:T(8,128)S(1)}, f32[64,128]{1,0:T(8,128)S(1)}, u32[]{:S(2)}, u32[]{:S(2)}) %collective-permute-start.2) | collective-permute-done | bytes 32800 | tf_op jit(solution)/shard_map/ppermute | solution.py:492
  15.4 0.0 collective-permute-done.3.cols_second
  15.4 4.2 %shard_map.168 = f32[3200,128]{1,0:T(8,128)} custom-call(f32[195,16,128]{2,1,0:T(8,128)S(1)} %get-tuple-element.32.tall, f32[64,128]{1,0:T(8,128)S(1)} %collective-permute-done.2.cols_first, f32[64,128]{1,0:T(8,128)S(1)} %collective-permute-done.3.cols_second, s32[1024,128]{1,0:T(8,128)S(1)} %get-tuple-element.35.slot_row, ...), custom_call_target="tpu_custom_call" | custom-call | flops 1000000 | bytes 3000000 | tf_op jit(solution)/shard_map/pallas_call | solution.py:51
  19.7 15.7 %all-to-all-start = ((f32[128,25,1,128]{3,2,1,0:T(1,128)}), f32[128,25,1,128]{3,2,1,0:T(1,128)S(1)}, u32[]{:S(2)}, u32[]{:S(2)}) async-start(f32[128,25,1,128]{3,2,1,0:T(1,128)} %bitcast.2), calls=%async_computation | async-start | bytes 3276800 | tf_op jit(solution)/shard_map/all_to_all | solution.py:539
  35.3 8.1 %shard_map.169 = (f32[64,8,128]{2,1,0:T(8,128)}, f32[64,8,128]{2,1,0:T(8,128)}) custom-call(f32[195,16,128]{2,1,0:T(8,128)S(1)} %get-tuple-element.32.tall, f32[64,128]{1,0:T(8,128)S(1)} %collective-permute-done.2.cols_first, f32[64,128]{1,0:T(8,128)S(1)} %collective-permute-done.3.cols_second), custom_call_target="tpu_custom_call" | custom-call | flops 100000000 | bytes 2000000 | tf_op jit(solution)/shard_map/pallas_call | solution.py:51
  43.4 1.9 %shard_map.170 = (f32[40,4096]{1,0:T(8,128)S(1)}, f32[40,4096]{1,0:T(8,128)S(1)}, f32[32,128]{1,0:T(8,128)S(1)}, f32[32,128]{1,0:T(8,128)S(1)}) custom-call(f32[40,4096]{1,0:T(8,128)} %enthalpy.1, f32[32,128]{1,0:T(8,128)} %bitcast.9, s32[32,128]{1,0:T(8,128)} %bitcast.10), custom_call_target="tpu_custom_call" | custom-call | flops 100000000 | bytes 2000000 | tf_op jit(solution)/shard_map/pallas_call | solution.py:51
  45.4 15.5 %all-to-all-done = f32[128,25,1,128]{3,2,1,0:T(1,128)S(1)} async-done(((f32[128,25,1,128]{3,2,1,0:T(1,128)}), f32[128,25,1,128]{3,2,1,0:T(1,128)S(1)}, u32[]{:S(2)}, u32[]{:S(2)}) %all-to-all-start) | async-done | bytes 1638432 | tf_op jit(solution)/shard_map/all_to_all | solution.py:539
  60.9 2.2 %shard_map.171 = (f32[40,4096]{1,0:T(8,128)}, f32[32,128]{1,0:T(8,128)}) custom-call(f32[3200,128]{1,0:T(8,128)S(1)} %bitcast.8, f32[32,128]{1,0:T(8,128)} %bitcast.11, f32[40,4096]{1,0:T(8,128)S(1)} %get-tuple-element.46.offset, f32[40,4096]{1,0:T(8,128)S(1)} %get-tuple-element.47.factor, f32[32,128]{1,0:T(8,128)S(1)} %get-tuple-element.48.pivot_end, ...), custom_call_target="tpu_custom_call" | custom-call | flops 1000000000 | bytes 4000000 | tf_op jit(solution)/shard_map/pallas_call | solution.py:51
Async XLA Ops:
  1.9 7.2 %collective-permute-start = (f32[392,128]{1,0:T(8,128)S(1)}, f32[392,128]{1,0:T(8,128)S(1)}, u32[]{:S(2)}, u32[]{:S(2)}) collective-permute-start(f32[392,128]{1,0:T(8,128)S(1)} %get-tuple-element.28), channel_id=1, source_target_pairs={{0,1},{1,0},{2,3},{3,2},{4,5},{5,4},{6,7},{7,6},{8,9},{9,8},{10,11... | collective-permute-start | bytes 602120 | tf_op jit(solution)/shard_map/ppermute | solution.py:492
  3.4 7.0 %collective-permute-start.1 = (f32[392,128]{1,0:T(8,128)S(1)}, f32[392,128]{1,0:T(8,128)S(1)}, u32[]{:S(2)}, u32[]{:S(2)}) collective-permute-start(f32[392,128]{1,0:T(8,128)S(1)} %get-tuple-element.31), channel_id=1, source_target_pairs={{1,2},{2,1},{3,4},{4,3},{5,6},{6,5},{9,10},{10,9},{11,12},{12,11},... | collective-permute-start | bytes 602120 | tf_op jit(solution)/shard_map/ppermute | solution.py:492
  12.6 2.8 %collective-permute-start.2 = (f32[64,128]{1,0:T(8,128)S(1)}, f32[64,128]{1,0:T(8,128)S(1)}, u32[]{:S(2)}, u32[]{:S(2)}) collective-permute-start(f32[64,128]{1,0:T(8,128)S(1)} %get-tuple-element.33), channel_id=1, source_target_pairs={{0,8},{8,0},{16,24},{24,16},{32,40},{40,32},{48,56},{56,48},{64,72... | collective-permute-start | bytes 98312 | tf_op jit(solution)/shard_map/ppermute | solution.py:492
  14.1 1.4 %collective-permute-start.3 = (f32[64,128]{1,0:T(8,128)S(1)}, f32[64,128]{1,0:T(8,128)S(1)}, u32[]{:S(2)}, u32[]{:S(2)}) collective-permute-start(f32[64,128]{1,0:T(8,128)S(1)} %get-tuple-element.34), channel_id=1, source_target_pairs={{8,16},{16,8},{24,32},{32,24},{40,48},{48,40},{56,64},{64,56},{72,... | collective-permute-start | bytes 98312 | tf_op jit(solution)/shard_map/ppermute | solution.py:492
  19.7 41.2 %all-to-all-start = ((f32[128,25,1,128]{3,2,1,0:T(1,128)}), f32[128,25,1,128]{3,2,1,0:T(1,128)S(1)}, u32[]{:S(2)}, u32[]{:S(2)}) async-start(f32[128,25,1,128]{3,2,1,0:T(1,128)} %bitcast.2), calls=%async_computation | async-start | bytes 3276800 | tf_op jit(solution)/shard_map/all_to_all | solution.py:539

commit v4 on v3

--- a/solution.py
+++ b/solution.py
@@ -4,6 +4,7 @@
 from jax.experimental import pallas as pl
 from jax.experimental.pallas import tpu as pltpu
 from jax.sharding import PartitionSpec as P
+
 
 mixing_rate = 0.2
 liquidus_slope = -0.0573
@@ -40,7 +41,7 @@
             arrays.append(pltpu.with_memory_space_constraint(array, pltpu.HBM))
             specs.append(part(block, index or (0,) * len(block)))
     if own_copies:
-        out_specs = pl.BlockSpec(memory_space=pltpu.HBM)
+        out_specs = jax.tree.map(lambda o: pl.BlockSpec(memory_space=pltpu.HBM), outs)
     else:
         out_specs = jax.tree.map(
             lambda o: part(o.shape, (0,) * len(o.shape))
@@ -69,68 +70,116 @@
     return pl.BlockSpec(tuple(shape), lambda i: tuple(index))
 
 
-def all_planes(temp, salt, wet, mix, friction, pressure):
+def even_on(axis):
+    return lax.axis_index(axis) % 2 == 0
+
+
+def all_rows_body(temp, salt, wet, mix, friction, pressure, first, second, centre):
+    even = even_on("gy")
+
+    def put(at, high, low):
+        first[at : at + 2, :] = jnp.where(even, high, low)
+        second[at : at + 2, :] = jnp.where(even, low, high)
+
+    at = 0
     for source in (temp, salt, wet):
         for k in range(levels):
-            yield source[k].astype(f32)
+            value = source[k].astype(f32)
+            centre[at // 2] = value
+            put(at, value[6:8, :], value[0:2, :])
+            at += 2
     for source in (mix, friction, pressure):
-        yield source[...]
-
-
-def even_on(axis):
-    return lax.axis_index(axis) % 2 == 0
-
-
-def row_pack(planes, first, second):
-    even = even_on("gy")
-    at = 0
-    for value in planes:
-        high, low = value[6:8, :], value[0:2, :]
-        first[at : at + 2, :] = jnp.where(even, high, low)
-        second[at : at + 2, :] = jnp.where(even, low, high)
+        centre[at // 2] = source[...]
+        put(at, source[6:8, :], source[0:2, :])
         at += 2
-    first[at:, :] = jnp.zeros((first.shape[0] - at, 128), f32)
-    second[at:, :] = jnp.zeros((first.shape[0] - at, 128), f32)
-
-
-def all_rows_body(temp, salt, wet, mix, friction, pressure, first, second):
-    row_pack(all_planes(temp, salt, wet, mix, friction, pressure), first, second)
-
-
-def col_pack(planes, groups, rows_first, rows_second, first, second, tall):
-    zeros = jnp.zeros((8, 128), f32)
-    half = lanes_of((16, 128)) // 2
+    put(at, jnp.zeros((2, 128), f32), jnp.zeros((2, 128), f32))
+
+
+def tall_plane(tall, at, value, rows_first, rows_second, place):
     at_first = jnp.where(even_on("gy"), 8, 14)
     at_second = 22 - at_first
-    for at, value in enumerate(planes):
-        tall[at, 0:8, :] = value
-        tall[at, 8:16, :] = zeros
-        tall[at, pl.ds(at_first, 2), :] = rows_first[2 * at : 2 * at + 2, :]
-        tall[at, pl.ds(at_second, 2), :] = rows_second[2 * at : 2 * at + 2, :]
-    even = even_on("gx")
+    tall[at, 0:8, :] = value
+    tall[at, 8:16, :] = jnp.zeros((8, 128), f32)
+    tall[at, pl.ds(at_first, 2), :] = rows_first[2 * place : 2 * place + 2, :]
+    tall[at, pl.ds(at_second, 2), :] = rows_second[2 * place : 2 * place + 2, :]
+
+
+plane_groups = (levels, levels, levels, 3)
+
+
+def own_columns(centre, low_side, high_side):
+    half = lanes_of((8, 128)) // 2
     start = 0
-    for group, count in enumerate(groups):
-        low = jnp.zeros((16, 128), f32)
-        high = jnp.zeros((16, 128), f32)
+    for group, count in enumerate(plane_groups):
+        low = jnp.zeros((8, 128), f32)
+        high = jnp.zeros((8, 128), f32)
         for k in range(count):
-            value = tall[start + k]
+            value = centre[start + k]
             here = half == k
             low = jnp.where(here, pltpu.roll(value, 2 * k, 1), low)
             high = jnp.where(here, pltpu.roll(value, (2 * k + 2) % 128, 1), high)
-        first[16 * group : 16 * group + 16, :] = jnp.where(even, high, low)
-        second[16 * group : 16 * group + 16, :] = jnp.where(even, low, high)
+        low_side[8 * group : 8 * group + 8, :] = low
+        high_side[8 * group : 8 * group + 8, :] = high
         start += count
+
+
+def all_cols_body(
+    centre, low_side, high_side, rows_first, rows_second, first, second, tall
+):
+    places = [field * levels + k for field in range(3) for k in range(few)]
+    places += [3 * levels + p for p in range(3)]
+    for at, place in enumerate(places):
+        tall_plane(tall, at, centre[place], rows_first, rows_second, place)
+
+    even_x = even_on("gx")
+    even_y = even_on("gy")
+    lane = lanes_of((8, 128))
+    row = lax.broadcasted_iota(jnp.int32, (8, 128), 0)
+    ahead = ((lane - row % 2) & 127) // 2 - row // 2
+
+    def put(at, low, high):
+        first[at : at + low.shape[0], :] = jnp.where(even_x, high, low)
+        second[at : at + low.shape[0], :] = jnp.where(even_x, low, high)
+
+    def row_columns(rows, start, count):
+        low = jnp.zeros((8, 128), f32)
+        high = jnp.zeros((8, 128), f32)
+        for k in range(0, count, 4):
+            value = rows[start + 2 * k : start + 2 * k + 8, :]
+            here = ahead == k
+            turned = pltpu.roll(value, 2 * k, 1, stride=1, stride_axis=0)
+            low = jnp.where(here, turned, low)
+            if 2 * k + 2 + 7 < 128:
+                turned = pltpu.roll(value, 2 * k + 2, 1, stride=1, stride_axis=0)
+            else:
+                turned = pltpu.roll(turned, 2, 1)
+            high = jnp.where(here, turned, high)
+        return tuple(
+            (
+                jnp.sum(jnp.where(row % 2 == 0, value, 0.0), axis=0, keepdims=True),
+                pltpu.roll(
+                    jnp.sum(jnp.where(row % 2 == 1, value, 0.0), axis=0, keepdims=True), 127, 1
+                ),
+            )
+            for value in (low, high)
+        )
+
+    for group in range(4):
+        own = slice(8 * group, 8 * group + 8)
+        put(16 * group, low_side[own, :], high_side[own, :])
+        put(16 * group + 8, jnp.zeros((8, 128), f32), jnp.zeros((8, 128), f32))
+        padded = levels if group < 3 else 4
+        one = row_columns(rows_first, 2 * group * levels, padded)
+        two = row_columns(rows_second, 2 * group * levels, padded)
+        for r in range(2):
+            pairs = tuple((a[r], b[r]) for a, b in zip(one, two))
+            put(16 * group + 8 + r, *(jnp.where(even_y, a, b) for a, b in pairs))
+            put(16 * group + 14 + r, *(jnp.where(even_y, b, a) for a, b in pairs))
 
 
 def sides_received(first, second):
     even = even_on("gx")
     return jnp.where(even, first, second), jnp.where(even, second, first)
-
-
-def all_cols_body(temp, salt, wet, mix, friction, pressure, rows_first, rows_second, first, second, tall):
-    planes = all_planes(temp, salt, wet, mix, friction, pressure)
-    groups = (levels, levels, levels, 3)
-    col_pack(planes, groups, rows_first, rows_second, first, second, tall)
 
 
 def extended(tall, from_right, from_left, k, dry=False):
@@ -194,13 +243,12 @@
 ):
     from_right, from_left = sides_received(cols_first[...], cols_second[...])
 
-    def plane(group, k):
+    def plane(p):
+        group, k = (p // few, p % few) if p < 3 * few else (3, p - 3 * few)
         rows = slice(16 * group, 16 * group + 16)
-        value = tall[group * levels + k]
-        return extended(value, from_right[rows], from_left[rows], k, group == 2)
-
-    planes = [plane(group, k) for group in range(3) for k in range(few)]
-    planes += [plane(3, place) for place in range(3)]
+        return extended(tall[p], from_right[rows], from_left[rows], k, group == 2)
+
+    planes = [plane(p) for p in range(12)]
     wets = planes[2 * few : 3 * few]
     mixing, rub, press = planes[9:12]
     first = mixing * (wets[0] * wets[1])
@@ -219,7 +267,7 @@
         near0 = spread(tops[field], links[0])
         near1 = spread(stepped[field][1], links[1])
         later.append(centre_of(near0 + first * (near1 - near0)))
-    heat_two, unused, base_two = shelf_melt(
+    heat_two, _, base_two = shelf_melt(
         later[0], later[1], centre_of(rub), centre_of(press), centre_of(wets[0])
     )
     melt = 0.5 * (centre_of(heat) / latent_ratio + heat_two / latent_ratio)
@@ -263,39 +311,65 @@
         leave(i).wait()
 
 
-def slot_body(owner, target, column, weight, slot_row, slot_lane, slot_weight, slot_target):
+def slot_body(
+    owner,
+    target,
+    column,
+    weight,
+    centre,
+    slot_row,
+    slot_lane,
+    slot_weight,
+    slot_target,
+    low_side,
+    high_side,
+):
+    own_columns(centre, low_side, high_side)
     count = owner.shape[1]
-    row = lax.broadcasted_iota(jnp.int32, (count, count), 0)
-    col = lax.broadcasted_iota(jnp.int32, (count, count), 1)
-    same = row == col
+    tiles = count // 128
+    row = lax.broadcasted_iota(jnp.int32, (128, 128), 0)
+    col = lax.broadcasted_iota(jnp.int32, (128, 128), 1)
+
+    def as_rows(value):
+        return [
+            jnp.sum(
+                jnp.where(row == col, value[:, 128 * t : 128 * t + 128], 0), axis=1, keepdims=True
+            )
+            for t in range(tiles)
+        ]
+
     owner_lane = owner[...]
-    alike = jnp.sum(jnp.where(same, owner_lane, 0), axis=1, keepdims=True) == owner_lane
-    rank_lane = jnp.sum(jnp.where(alike & (row < col), 1, 0), axis=0, keepdims=True)
-    rank_row = jnp.sum(jnp.where(alike & (col < row), 1, 0), axis=1, keepdims=True)
-    target_row = jnp.sum(jnp.where(same, target[...], 0), axis=1, keepdims=True)
+    owner_row = as_rows(owner_lane)
+    ranks = []
+    for t in range(tiles):
+        here = owner_lane[:, 128 * t : 128 * t + 128]
+        seen = jnp.where((owner_row[t] == here) & (row < col), 1, 0)
+        for before in range(t):
+            seen = seen + jnp.where(owner_row[before] == here, 1, 0)
+        ranks.append(jnp.sum(seen, axis=0, keepdims=True))
+    rank_lane = jnp.concatenate(ranks, axis=1)
+    rank_row = jnp.concatenate(as_rows(rank_lane), axis=0)
+    target_row = jnp.concatenate(as_rows(target[...]), axis=0)
     slot = owner_lane * slots + rank_lane
     total = slot_row.shape[0]
     pick = jnp.where(lax.broadcasted_iota(jnp.int32, (total, count), 0) == slot, 1.0, 0.0)
     value = weight[...]
     high = value.astype(bf16)
-    rest = value - high.astype(f32)
-    middle = rest.astype(bf16)
-    low = (rest - middle.astype(f32)).astype(bf16)
+    low = (value - high.astype(f32)).astype(bf16)
     places = column[...]
     table = jnp.concatenate(
         [
             high,
-            middle,
             low,
-            (places // 128).astype(f32).astype(bf16),
-            (places % 128).astype(f32).astype(bf16),
+            (places >> 7).astype(f32).astype(bf16),
+            (places & 127).astype(f32).astype(bf16),
         ],
         axis=1,
     )
     sorted_ = jnp.dot(pick.astype(bf16), table, preferred_element_type=f32)
-    slot_weight[...] = sorted_[:, 0:128] + sorted_[:, 128:256] + sorted_[:, 256:384]
-    slot_row[...] = sorted_[:, 384:512].astype(jnp.int32)
-    slot_lane[...] = sorted_[:, 512:640].astype(jnp.int32)
+    slot_weight[...] = sorted_[:, 0:128] + sorted_[:, 128:256]
+    slot_row[...] = sorted_[:, 256:384].astype(jnp.int32)
+    slot_lane[...] = sorted_[:, 384:512].astype(jnp.int32)
     lane = lax.broadcasted_iota(jnp.int32, (count, 128), 1)
     spot = jnp.where(rank_row == lane % slots, target_row, 0).astype(f32).astype(bf16)
     holds = jnp.where(lax.broadcasted_iota(jnp.int32, (128, count), 0) == owner_lane, 1.0, 0.0)
@@ -303,7 +377,9 @@
 
 
 def ocean_body(
-    tall,
+    centre,
+    rows_first,
+    rows_second,
     cols_first,
     cols_second,
     new_temp,
@@ -314,7 +390,10 @@
     later,
     from_right,
     from_left,
+    tall,
 ):
+    for at in range(3 * levels + 3):
+        tall_plane(tall, at, centre[at], rows_first, rows_second, at)
     from_right[...], from_left[...] = sides_received(cols_first[...], cols_second[...])
     for end in (0, levels + 1):
         wets[end] = jnp.zeros((16, 256), f32)
@@ -360,7 +439,7 @@
             value_over = over * (value - near[field, k])
             once.append(value + value_under - value_over)
         if top:
-            heat, brine, unused = shelf_melt(once[0], once[1], rub, press, water)
+            heat, brine, _ = shelf_melt(once[0], once[1], rub, press, water)
             once = [once[0] - relax_rate * heat, once[1] - relax_rate * brine]
         for field in range(2):
             change = jnp.zeros((8, 128), f32)
@@ -381,9 +460,7 @@
             value_over = over * (value - later[field, k])
             done.append(value + value_under - value_over)
         if top:
-            heat, brine, unused = shelf_melt(
-                done[0], done[1], centre_of(rub), centre_of(press), water
-            )
+            heat, brine, _ = shelf_melt(done[0], done[1], centre_of(rub), centre_of(press), water)
             done = [done[0] - relax_rate * heat, done[1] - relax_rate * brine]
         new_temp[k] = done[0]
         new_salt[k] = done[1]
@@ -403,7 +480,10 @@
     finish_level(0, True)
 
 
-def column_body(enthalpy, surface, transition, offset, factor, pivot_end, side_end):
+def column_body(
+    enthalpy, surface, transition, area, offset, factor, pivot_end, side_end, per_area
+):
+    per_area[...] = 1.0 / area[...]
     count = enthalpy.shape[0]
     side = enthalpy[...].reshape(count, 32, 128)
     change_at = transition[...]
@@ -432,7 +512,19 @@
     factor[...] = jnp.stack(factors[::-1]).reshape(count, 4096)
 
 
-def collect_body(got, area, offset, factor, pivot_end, side_end, new_enthalpy, melt):
+def collect_body(
+    got,
+    offset,
+    factor,
+    pivot_end,
+    side_end,
+    per_area,
+    new_enthalpy,
+    melt,
+    held,
+    held_melt,
+    sems,
+):
     sums = jnp.zeros((32, 384), f32)
     lane = lax.broadcasted_iota(jnp.int32, (1, 128), 1) // slots
     wanted = lax.broadcasted_iota(jnp.int32, (32, 128), 0).astype(f32)
@@ -447,18 +539,25 @@
         hot = jnp.where(wanted == target, 1.0, 0.0).astype(bf16)
         value = jnp.concatenate([jnp.concatenate(p, axis=0) for p in parts], axis=1)
         high = value.astype(bf16)
-        rest = value - high.astype(f32)
-        middle = rest.astype(bf16)
-        low = (rest - middle.astype(f32)).astype(bf16)
-        for piece in (high, middle, low):
+        low = (value - high.astype(f32)).astype(bf16)
+        for piece in (high, low):
             sums = sums + jnp.dot(hot, piece, preferred_element_type=f32)
-    size = area[...]
-    melt[...] = sums[:, 0:128] / size
-    base_sum = sums[:, 128:256] / size
-    cover_sum = sums[:, 256:384] / size
+    scale = per_area[...]
+    held_melt[...] = sums[:, 0:128] * scale
+    copies = [pltpu.make_async_copy(held_melt, melt, sems.at[0])]
+    copies[0].start()
+    base_sum = sums[:, 128:256] * scale
+    cover_sum = sums[:, 256:384] * scale
     last = (side_end[...] + base_sum) / (pivot_end[...] + cover_sum)
     last = last.reshape(1, 4096)
-    new_enthalpy[...] = offset[...] + factor[...] * last
+    for k in range(0, held.shape[0], 8):
+        rows = pl.ds(k, 8)
+        held[rows, :] = offset[rows, :] + factor[rows, :] * last
+        copy = pltpu.make_async_copy(held.at[rows], new_enthalpy.at[rows], sems.at[1 + k // 8])
+        copy.start()
+        copies.append(copy)
+    for copy in copies:
+        copy.wait()
 
 
 def local(
@@ -489,28 +588,40 @@
     def exchange(first, second, axis, count):
         pairs = [(i, i ^ 1) for i in range(count)]
         later = [(i + 1, (i ^ 1) + 1) for i in range(count - 2)]
-        return lax.ppermute(first, axis, pairs), lax.ppermute(second, axis, later)
-
-    rows_first, rows_second = call(
-        all_rows_body, (chip(halo_rows, 128), chip(halo_rows, 128)), ocean, cost=(10**5, 10**6)
+        first = lax.ppermute(first, axis, pairs)
+        return first, lax.ppermute(second, axis, later)
+
+    rows_first, rows_second, centre = call(
+        all_rows_body,
+        (chip(halo_rows, 128), chip(halo_rows, 128), chip(3 * levels + 3, 8, 128)),
+        ocean,
+        cost=(10**5, 10**6),
     )
     rows_first, rows_second = exchange(rows_first, rows_second, "gy", count_y)
-    slot_row, slot_lane, slot_weight, slot_target = call(
+    slot_row, slot_lane, slot_weight, slot_target, low_side, high_side = call(
         slot_body,
         (
             chip(devices * slots, 128, dtype=jnp.int32),
             chip(devices * slots, 128, dtype=jnp.int32),
             chip(devices * slots, 128),
             chip(devices, 128),
+            chip(32, 128),
+            chip(32, 128),
         ),
-        (block_owner.reshape(1, -1), block_target.reshape(1, -1), pair_column, pair_weight),
+        (
+            block_owner.reshape(1, -1),
+            block_target.reshape(1, -1),
+            pair_column,
+            pair_weight,
+            Near(centre),
+        ),
         cost=(2 * 10**9, 3 * 10**6),
     )
     rows_first, slot_target = lax.optimization_barrier((rows_first, slot_target))
     cols_first, cols_second, tall = call(
         all_cols_body,
-        (chip(64, 128), chip(64, 128), chip(3 * levels + 3, 16, 128)),
-        ocean + (Near(rows_first), Near(rows_second)),
+        (chip(64, 128), chip(64, 128), chip(12, 16, 128)),
+        tuple(Near(a) for a in (centre, low_side, high_side, rows_first, rows_second)),
         cost=(10**5, 10**6),
     )
     cols_first, cols_second = exchange(cols_first, cols_second, "gx", count_x)
@@ -546,7 +657,7 @@
     new_temp, new_salt = call(
         ocean_body,
         (shape(ocean_temp.shape, f32), shape(ocean_salt.shape, f32)),
-        (Near(tall), Near(cols_first), Near(cols_second)),
+        tuple(Near(a) for a in (centre, rows_first, rows_second, cols_first, cols_second)),
         [
             pltpu.VMEM((2, levels + 2, 16, 256), f32),
             pltpu.VMEM((levels + 2, 16, 256), f32),
@@ -554,28 +665,33 @@
             pltpu.VMEM((2, levels + 2, 8, 128), f32),
             pltpu.VMEM((64, 128), f32),
             pltpu.VMEM((64, 128), f32),
+            pltpu.VMEM((3 * levels + 3, 16, 128), f32),
         ],
         cost=(10**8, 2 * 10**6),
     )
     new_temp, surface_enthalpy = lax.optimization_barrier((new_temp, surface_enthalpy))
-    offset, factor, pivot_end, side_end = call(
+    offset, factor, pivot_end, side_end, per_area = call(
         column_body,
-        (chip(*enthalpy.shape), chip(*enthalpy.shape), chip(32, 128), chip(32, 128)),
-        (enthalpy, surface_enthalpy.reshape(32, 128), transition_layer.reshape(32, 128)),
+        (chip(*enthalpy.shape), chip(*enthalpy.shape)) + (chip(32, 128),) * 3,
+        (
+            enthalpy,
+            surface_enthalpy.reshape(32, 128),
+            transition_layer.reshape(32, 128),
+            column_area.reshape(32, 128),
+        ),
         cost=(10**8, 2 * 10**6),
     )
     new_enthalpy, melt = call(
         collect_body,
         (shape(enthalpy.shape, f32), shape((32, 128), f32)),
-        (
-            Near(got),
-            column_area.reshape(32, 128),
-            Near(offset),
-            Near(factor),
-            Near(pivot_end),
-            Near(side_end),
-        ),
+        tuple(Near(a) for a in (got, offset, factor, pivot_end, side_end, per_area)),
+        [
+            pltpu.VMEM(enthalpy.shape, f32),
+            pltpu.VMEM((32, 128), f32),
+            pltpu.SemaphoreType.DMA((1 + enthalpy.shape[0] // 8,)),
+        ],
         cost=(10**9, 4 * 10**6),
+        own_copies=True,
     )
     return new_temp, new_salt, new_enthalpy, melt.reshape(-1)
 

time: 63.4 us -> 60.9 us (0.961)
  Pallas kernels: 22.6 us -> 20.2 us
    pallas_call x7, Pallas kernels: 22.6 us -> 20.2 us  [call(): pl.pallas_call(body, out_shape=outs, grid=(1,), in_specs=specs, out_specs...]
  transfers between devices with their start and end apart: 5 -> 5, of which waited for: 3 -> 3; matrix products, arithmetic and copies ran while one was open for 0% -> 0% of each run, Pallas kernels for 20% -> 21%
where the time goes in v4:
time: 60.9 us; the launch traced here: 60.6 us
  starting transfers between devices  22.1 us (36%)
  Pallas kernels  20.2 us (33%)
  waiting for transfers between devices  17.6 us (29%)
  between operations  0.7 us (1%)
    pallas_call x7, Pallas kernels, call(): pl.pallas_call(body, out_shape=outs, grid=(1,), in_specs=specs, out_specs...  20.2 us
    all_to_all x1, starting transfers between devices, local(): lax.all_to_all(send.reshape(devices, chunk, 1, 128), ('gx', 'gy'), split_...  15.4 us
    all_to_all x1, waiting for transfers between devices, local(): lax.all_to_all(send.reshape(devices, chunk, 1, 128), ('gx', 'gy'), split_...  15.2 us
    ppermute x2, starting transfers between devices, exchange(): return (first, lax.ppermute(second, axis, later))  3.78 us
    ppermute x2, starting transfers between devices, exchange(): first = lax.ppermute(first, axis, pairs)  2.95 us
    ppermute x2, waiting for transfers between devices, exchange(): return (first, lax.ppermute(second, axis, later))  1.66 us
  transfers between devices with their start and end apart: 5, of which 3 were waited for; matrix products, arithmetic and copies ran while one was open for 0% of the time, Pallas kernels for 21%

profile of v4, /device:TPU:1, one launch (start us, length us, event | category | flops | bytes accessed | tf_op | source)
XLA Modules:
  0.0 60.6 jit_solution(12987285717022454076)
XLA Ops:
  0.6 1.3 %shard_map.165 = (f32[392,128]{1,0:T(8,128)S(1)}, f32[392,128]{1,0:T(8,128)S(1)}, f32[195,8,128]{2,1,0:T(8,128)S(1)}) custom-call(f32[64,8,128]{2,1,0:T(8,128)} %temp.1, f32[64,8,128]{2,1,0:T(8,128)} %salt.1, s32[64,8,128]{2,1,0:T(8,128)} %wet.1, f32[8,128]{1,0:T(8,128)} %mix.1, f32[8,128]{1,0:T(8,128)} %friction.1, f32[8,128]{1,0:T(8,128)} %pressure.1), custom_call_target="tpu_custom_call" | custom-call | flops 100000 | bytes 1000000 | tf_op jit(solution)/shard_map/pallas_call | solution.py:52
  1.9 1.5 %collective-permute-start = (f32[392,128]{1,0:T(8,128)S(1)}, f32[392,128]{1,0:T(8,128)S(1)}, u32[]{:S(2)}, u32[]{:S(2)}) collective-permute-start(f32[392,128]{1,0:T(8,128)S(1)} %get-tuple-element.33), channel_id=1, source_target_pairs={{0,1},{1,0},{2,3},{3,2},{4,5},{5,4},{6,7},{7,6},{8,9},{9,8},{10,11... | collective-permute-start | bytes 602120 | tf_op jit(solution)/shard_map/ppermute | solution.py:591
  3.4 3.1 %collective-permute-start.1 = (f32[392,128]{1,0:T(8,128)S(1)}, f32[392,128]{1,0:T(8,128)S(1)}, u32[]{:S(2)}, u32[]{:S(2)}) collective-permute-start(f32[392,128]{1,0:T(8,128)S(1)} %get-tuple-element.36), channel_id=1, source_target_pairs={{1,2},{2,1},{3,4},{4,3},{5,6},{6,5},{9,10},{10,9},{11,12},{12,11},... | collective-permute-start | bytes 602120 | tf_op jit(solution)/shard_map/ppermute | solution.py:592
  6.5 2.5 %shard_map.166 = (s32[1024,128]{1,0:T(8,128)S(1)}, s32[1024,128]{1,0:T(8,128)S(1)}, f32[1024,128]{1,0:T(8,128)S(1)}, f32[128,128]{1,0:T(8,128)S(1)}, f32[32,128]{1,0:T(8,128)S(1)}, /*index=5*/f32[32,128]{1,0:T(8,128)S(1)}) custom-call(s32[1,512]{1,0:T(1,128)} %bitcast.12, s32[1,512]{1,0:T(1,128)} %bitcast.13, s32[512,128]{1,0:T(8,128)} %column.1, ...), custom_call_target="tpu_custom_call" | custom-call | flops 2000000000 | bytes 3000000 | tf_op jit(solution)/shard_map/pallas_call | solution.py:52
  9.0 0.0 collective-permute-done.rows_first
  9.1 1.7 %collective-permute-done.1.rows_second = f32[392,128]{1,0:T(8,128)S(1)} collective-permute-done((f32[392,128]{1,0:T(8,128)S(1)}, f32[392,128]{1,0:T(8,128)S(1)}, u32[]{:S(2)}, u32[]{:S(2)}) %collective-permute-start.1) | collective-permute-done | bytes 200736 | tf_op jit(solution)/shard_map/ppermute | solution.py:592
  10.7 0.5 shard_map.167
  11.2 1.5 %collective-permute-start.2 = (f32[64,128]{1,0:T(8,128)S(1)}, f32[64,128]{1,0:T(8,128)S(1)}, u32[]{:S(2)}, u32[]{:S(2)}) collective-permute-start(f32[64,128]{1,0:T(8,128)S(1)} %get-tuple-element.40), channel_id=1, source_target_pairs={{0,8},{8,0},{16,24},{24,16},{32,40},{40,32},{48,56},{56,48},{64,72... | collective-permute-start | bytes 98312 | tf_op jit(solution)/shard_map/ppermute | solution.py:591
  12.7 0.7 %collective-permute-start.3 = (f32[64,128]{1,0:T(8,128)S(1)}, f32[64,128]{1,0:T(8,128)S(1)}, u32[]{:S(2)}, u32[]{:S(2)}) collective-permute-start(f32[64,128]{1,0:T(8,128)S(1)} %get-tuple-element.41), channel_id=1, source_target_pairs={{8,16},{16,8},{24,32},{32,24},{40,48},{48,40},{56,64},{64,56},{72,... | collective-permute-start | bytes 98312 | tf_op jit(solution)/shard_map/ppermute | solution.py:592
  13.4 0.7 %collective-permute-done.2.cols_first = f32[64,128]{1,0:T(8,128)S(1)} collective-permute-done((f32[64,128]{1,0:T(8,128)S(1)}, f32[64,128]{1,0:T(8,128)S(1)}, u32[]{:S(2)}, u32[]{:S(2)}) %collective-permute-start.2) | collective-permute-done | bytes 32800 | tf_op jit(solution)/shard_map/ppermute | solution.py:591
  14.1 0.0 collective-permute-done.3.cols_second
  14.1 4.2 %shard_map.168 = f32[3200,128]{1,0:T(8,128)} custom-call(f32[12,16,128]{2,1,0:T(8,128)S(1)} %get-tuple-element.39.tall, f32[64,128]{1,0:T(8,128)S(1)} %collective-permute-done.2.cols_first, f32[64,128]{1,0:T(8,128)S(1)} %collective-permute-done.3.cols_second, s32[1024,128]{1,0:T(8,128)S(1)} %get-tuple-element.42.slot_row, ...), custom_call_target="tpu_custom_call" | custom-call | flops 1000000 | bytes 3000000 | tf_op jit(solution)/shard_map/pallas_call | solution.py:52
  18.3 15.4 %all-to-all-start = ((f32[128,25,1,128]{3,2,1,0:T(1,128)}), f32[128,25,1,128]{3,2,1,0:T(1,128)S(1)}, u32[]{:S(2)}, u32[]{:S(2)}) async-start(f32[128,25,1,128]{3,2,1,0:T(1,128)} %bitcast.2), calls=%async_computation | async-start | bytes 3276800 | tf_op jit(solution)/shard_map/all_to_all | solution.py:650
  33.7 8.4 %shard_map.169 = (f32[64,8,128]{2,1,0:T(8,128)}, f32[64,8,128]{2,1,0:T(8,128)}) custom-call(f32[195,8,128]{2,1,0:T(8,128)S(1)} %get-tuple-element.32.centre, f32[392,128]{1,0:T(8,128)S(1)} %collective-permute-done.rows_first, f32[392,128]{1,0:T(8,128)S(1)} %collective-permute-done.1.rows_second, f32[64,128]{1,0:T(8,128)S(1)} %collective-permute-done.2.cols_first, ...), custom_call_target="tpu_custom_call" | custom-call | flops 100000000 | bytes 2000000 | tf_op jit(solution)/shard_map/pallas_call | solution.py:52
  42.1 1.9 %shard_map.170 = (f32[40,4096]{1,0:T(8,128)S(1)}, f32[40,4096]{1,0:T(8,128)S(1)}, f32[32,128]{1,0:T(8,128)S(1)}, f32[32,128]{1,0:T(8,128)S(1)}, f32[32,128]{1,0:T(8,128)S(1)}) custom-call(f32[40,4096]{1,0:T(8,128)} %enthalpy.1, f32[32,128]{1,0:T(8,128)} %bitcast.9, s32[32,128]{1,0:T(8,128)} %bitcast.10, f32[32,128]{1,0:T(8,128)} %bitcast.11), custom_call_target="tpu_custom_call" | custom-call | flops 100000000 | bytes 2000000 | tf_op jit(solution)/shard_map/pallas_call | solution.py:52
  44.0 15.2 %all-to-all-done = f32[128,25,1,128]{3,2,1,0:T(1,128)S(1)} async-done(((f32[128,25,1,128]{3,2,1,0:T(1,128)}), f32[128,25,1,128]{3,2,1,0:T(1,128)S(1)}, u32[]{:S(2)}, u32[]{:S(2)}) %all-to-all-start) | async-done | bytes 1638432 | tf_op jit(solution)/shard_map/all_to_all | solution.py:650
  59.2 1.4 %shard_map.171 = (f32[40,4096]{1,0:T(8,128)}, f32[32,128]{1,0:T(8,128)}) custom-call(f32[3200,128]{1,0:T(8,128)S(1)} %bitcast.8, f32[40,4096]{1,0:T(8,128)S(1)} %get-tuple-element.53.offset, f32[40,4096]{1,0:T(8,128)S(1)} %get-tuple-element.54.factor, f32[32,128]{1,0:T(8,128)S(1)} %get-tuple-element.55.pivot_end, f32[32,128]{1,0:T(8,128)S(1)} %get-tuple-element.56.side_end, ...), custom_call_target="tpu_custom_call" | custom-call | flops 1000000000 | bytes 4000000 | tf_op jit(solution)/shard_map/pallas_call | solution.py:52
Async XLA Ops:
  1.9 7.1 %collective-permute-start = (f32[392,128]{1,0:T(8,128)S(1)}, f32[392,128]{1,0:T(8,128)S(1)}, u32[]{:S(2)}, u32[]{:S(2)}) collective-permute-start(f32[392,128]{1,0:T(8,128)S(1)} %get-tuple-element.33), channel_id=1, source_target_pairs={{0,1},{1,0},{2,3},{3,2},{4,5},{5,4},{6,7},{7,6},{8,9},{9,8},{10,11... | collective-permute-start | bytes 602120 | tf_op jit(solution)/shard_map/ppermute | solution.py:591
  3.4 7.3 %collective-permute-start.1 = (f32[392,128]{1,0:T(8,128)S(1)}, f32[392,128]{1,0:T(8,128)S(1)}, u32[]{:S(2)}, u32[]{:S(2)}) collective-permute-start(f32[392,128]{1,0:T(8,128)S(1)} %get-tuple-element.36), channel_id=1, source_target_pairs={{1,2},{2,1},{3,4},{4,3},{5,6},{6,5},{9,10},{10,9},{11,12},{12,11},... | collective-permute-start | bytes 602120 | tf_op jit(solution)/shard_map/ppermute | solution.py:592
  11.2 2.8 %collective-permute-start.2 = (f32[64,128]{1,0:T(8,128)S(1)}, f32[64,128]{1,0:T(8,128)S(1)}, u32[]{:S(2)}, u32[]{:S(2)}) collective-permute-start(f32[64,128]{1,0:T(8,128)S(1)} %get-tuple-element.40), channel_id=1, source_target_pairs={{0,8},{8,0},{16,24},{24,16},{32,40},{40,32},{48,56},{56,48},{64,72... | collective-permute-start | bytes 98312 | tf_op jit(solution)/shard_map/ppermute | solution.py:591
  12.7 1.4 %collective-permute-start.3 = (f32[64,128]{1,0:T(8,128)S(1)}, f32[64,128]{1,0:T(8,128)S(1)}, u32[]{:S(2)}, u32[]{:S(2)}) collective-permute-start(f32[64,128]{1,0:T(8,128)S(1)} %get-tuple-element.41), channel_id=1, source_target_pairs={{8,16},{16,8},{24,32},{32,24},{40,48},{48,40},{56,64},{64,56},{72,... | collective-permute-start | bytes 98312 | tf_op jit(solution)/shard_map/ppermute | solution.py:592
  18.3 40.9 %all-to-all-start = ((f32[128,25,1,128]{3,2,1,0:T(1,128)}), f32[128,25,1,128]{3,2,1,0:T(1,128)S(1)}, u32[]{:S(2)}, u32[]{:S(2)}) async-start(f32[128,25,1,128]{3,2,1,0:T(1,128)} %bitcast.2), calls=%async_computation | async-start | bytes 3276800 | tf_op jit(solution)/shard_map/all_to_all | solution.py:650
